TPU v7x, 32 devices: a whole 2x2x4 slice. The times are simulated.
32 devices in a mesh: dp: 4 (over z), row: 4 (over y, x), col: 2 (over core).
Axes of the slice: x: 2, y: 2, z: 4, core: 2. Of those that a mesh axis runs over, the one named last changes fastest.
Arguments:
- hidden_in: bfloat16 [32768, 768], P(('dp', 'row'), 'col'), may hold values from -6 to 6
- doc_ids: int32 [16, 2048], P(('dp', 'row')), may hold values from 0 to 3, never falling along the last dimension, each value on 1 to 1024 neighbouring positions
- norm_gain: bfloat16 [768], P('col'), may hold values from 0.5 to 1.5
- proj_gate: bfloat16 [768, 1536], P('row', 'col'), may hold values from -0.21875 to 0.21875
- proj_inner: bfloat16 [768, 1536], P('row', 'col'), may hold values from -0.21875 to 0.21875
- proj_states: bfloat16 [768, 256], P('row'), may hold values from -0.21875 to 0.21875
- proj_step: bfloat16 [768, 24], P('row', 'col'), may hold values from -0.21875 to 0.21875
- conv_inner_weight: float32 [4, 1536], P(None, 'col'), may hold values from -3 to 3
- conv_inner_bias: float32 [1536], P('col'), may hold values from -3 to 3
- conv_state_weight: float32 [4, 256], replicated, may hold values from -3 to 3
- conv_state_bias: float32 [256], replicated, may hold values from -3 to 3
- step_bias: float32 [24], P('col'), may hold values from -6 to -2.5
- decay_log: float32 [24], P('col'), may hold values from 0 to 2.77
- skip_gain: float32 [24], P('col'), may hold values from 0.5 to 1.5
- gated_gain: float32 [1536], P('col'), may hold values from 0.5 to 1.5
- proj_out: bfloat16 [1536, 768], P('col', 'row'), may hold values from -0.15625 to 0.15625
- out_grad: bfloat16 [32768, 768], P(('dp', 'row'), 'col'), may hold values from -6 to 6
Outputs:
- block_out: bfloat16 [32768, 768], P(('dp', 'row'), 'col')
- grad_hidden: float32 [32768, 768], P(('dp', 'row'), 'col')
- grad_norm_gain: float32 [768], P('col')
- grad_proj_gate: float32 [768, 1536], P('row', 'col')
- grad_proj_inner: float32 [768, 1536], P('row', 'col')
- grad_proj_states: float32 [768, 256], P('row')
- grad_proj_step: float32 [768, 24], P('row', 'col')
- grad_conv_inner_weight: float32 [4, 1536], P(None, 'col')
- grad_conv_inner_bias: float32 [1536], P('col')
- grad_conv_state_weight: float32 [4, 256], replicated
- grad_conv_state_bias: float32 [256], replicated
- grad_step_bias: float32 [24], P('col')
- grad_decay_log: float32 [24], P('col')
- grad_skip_gain: float32 [24], P('col')
- grad_gated_gain: float32 [1536], P('col')
- grad_proj_out: float32 [1536, 768], P('col', 'row')
Inputs may be any that keep to these rules, and one draw needn't show every extreme that they name: `doc_ids`: along each pack the numbers never fall, and each run of one number is 1 to 1024 tokens long.
All inputs are finite; a program needn't handle non-finite values.
Results may differ from a plain program's by a relative error of at most 0.012.
Values may be sent and summed in bfloat16 or wider, within the bound.
A program may use at most 192 MiB of HBM per device.

v0:
```python
from functools import partial

import jax
import jax.numpy as jnp
from jax import lax
from jax.sharding import PartitionSpec as P

KW = 4
BLOCK = 256


epsilon = 1e-05
highest = lax.Precision.HIGHEST
scan_precision = lax.Precision.HIGH


def round_keep(values):
    rounded = values.astype(jnp.bfloat16).astype(jnp.float32)
    return values + lax.stop_gradient(rounded - values)


def shift_masks(doc_row):
    rows_list = [jnp.ones(doc_row.shape, jnp.float32)]
    for offset in range(1, KW):
        earlier = jnp.concatenate([jnp.full((offset,), -1, jnp.int32), doc_row[:-offset]])
        rows_list.append((earlier == doc_row).astype(jnp.float32))
    return jnp.stack(rows_list)


def conv_mix(values, weight, bias_row, near_masks):
    taps = weight.shape[0]
    conv_sum = bias_row[None, :] + weight[taps - 1][None, :] * values
    for offset in range(1, taps):
        pad_rows = jnp.zeros((offset, values.shape[1]), jnp.float32)
        shifted = jnp.concatenate([pad_rows, values[:-offset]], axis=0)
        conv_sum = (
            conv_sum + weight[taps - 1 - offset][None, :] * shifted * near_masks[offset][:, None]
        )
    return jax.nn.silu(conv_sum)


def ssd_scan(inner_vals, write_vec, read_vec, log_rate, step_size, doc_row, skip_gain):
    tokens, head_count, head_dim = inner_vals.shape
    blocks = tokens // BLOCK
    rate_heads = jnp.transpose(log_rate.reshape(blocks, BLOCK, head_count), (0, 2, 1))
    step_heads = jnp.transpose(step_size.reshape(blocks, BLOCK, head_count), (0, 2, 1))
    pieces = (
        inner_vals.reshape(blocks, BLOCK, head_count, head_dim),
        write_vec.reshape(blocks, BLOCK, -1),
        read_vec.reshape(blocks, BLOCK, -1),
        rate_heads,
        step_heads,
        doc_row.reshape(blocks, BLOCK),
    )
    positions = jnp.arange(BLOCK)
    lower_tri = positions[:, None] >= positions[None, :]

    def one_block(carry_in, block_data):
        carried, last_doc = carry_in
        inner_blk, write_blk, read_blk, rate_blk, step_blk, doc_blk = block_data
        cumulative = jnp.cumsum(rate_blk, axis=1)
        allowed = lower_tri & (doc_blk[:, None] == doc_blk[None, :])
        allowed_wide = allowed[None, :, :]
        log_gaps = cumulative[:, :, None] - cumulative[:, None, :]
        decay_mat = jnp.exp(jnp.where(allowed_wide, log_gaps, 0.0)) * allowed_wide.astype(
            jnp.float32
        )
        scores = jnp.dot(read_blk, write_blk.T, precision=scan_precision)
        mixing = scores[None, :, :] * decay_mat * step_blk[:, None, :]
        local_out = jnp.einsum("hts,shp->thp", mixing, inner_blk, precision=scan_precision)
        enter_scale = (doc_blk == last_doc).astype(jnp.float32)[None, :] * jnp.exp(cumulative)
        from_state = (
            jnp.einsum("tn,hpn->thp", read_blk, carried, precision=scan_precision)
            * enter_scale.T[:, :, None]
        )
        result = local_out + from_state + skip_gain[None, :, None] * inner_blk
        final_doc = doc_blk[BLOCK - 1]
        keep_state = (final_doc == last_doc).astype(jnp.float32)
        weights_tail = (
            jnp.exp(cumulative[:, BLOCK - 1 :] - cumulative)
            * step_blk
            * (doc_blk == final_doc).astype(jnp.float32)[None, :]
        )
        update = jnp.einsum(
            "hs,shp,sn->hpn", weights_tail, inner_blk, write_blk, precision=scan_precision
        )
        carried = keep_state * jnp.exp(cumulative[:, BLOCK - 1])[:, None, None] * carried + update
        return ((carried, final_doc), result)

    start_carry = (
        jnp.zeros((head_count, head_dim, write_vec.shape[1]), jnp.float32),
        jnp.array(-1, jnp.int32),
    )
    final_carry, outputs = lax.scan(jax.checkpoint(one_block), start_carry, pieces)
    return outputs.reshape(tokens, head_count, head_dim)


def mixer_core(
    near_masks,
    doc_row,
    gate_in,
    inner_in,
    state_in,
    step_in,
    conv_inner_weight,
    conv_inner_bias,
    conv_state_weight,
    conv_state_bias,
    step_bias,
    decay_log,
    skip_gain,
):
    tokens = gate_in.shape[0]
    head_count = step_in.shape[1]
    states = state_in.shape[1] // 2
    inner_vals = round_keep(conv_mix(inner_in, conv_inner_weight, conv_inner_bias, near_masks))
    state_vals = round_keep(conv_mix(state_in, conv_state_weight, conv_state_bias, near_masks))
    step_size = jax.nn.softplus(step_in + step_bias[None, :])
    log_rate = -jnp.exp(decay_log)[None, :] * step_size
    mixed_out = ssd_scan(
        inner_vals.reshape(tokens, head_count, -1),
        state_vals[:, :states],
        state_vals[:, states:],
        log_rate,
        step_size,
        doc_row,
        skip_gain,
    )
    return mixed_out.reshape(tokens, -1) * jax.nn.silu(gate_in)


def body(
    hidden_in,
    doc_ids,
    norm_gain,
    proj_gate,
    proj_inner,
    proj_states,
    proj_step,
    conv_inner_weight,
    conv_inner_bias,
    conv_state_weight,
    conv_state_bias,
    step_bias,
    decay_log,
    skip_gain,
    gated_gain,
    proj_out,
    out_grad,
):
    doc_row = doc_ids[0]
    full_hidden, full_grad, full_gain = (
        lax.all_gather(hidden_in, "col", axis=1, tiled=True),
        lax.all_gather(out_grad, "col", axis=1, tiled=True),
        lax.all_gather(norm_gain, "col", axis=0, tiled=True),
    )
    gate_all, inner_all, states_all, step_all, out_all = (
        lax.all_gather(proj_gate, "row", axis=0, tiled=True),
        lax.all_gather(proj_inner, "row", axis=0, tiled=True),
        lax.all_gather(proj_states, "row", axis=0, tiled=True),
        lax.all_gather(proj_step, "row", axis=0, tiled=True),
        lax.all_gather(proj_out, "row", axis=1, tiled=True),
    )
    model_width = full_hidden.shape[1]
    hidden_float = full_hidden.astype(jnp.float32)
    inv_in = lax.rsqrt(jnp.mean(hidden_float * hidden_float, axis=1, keepdims=True) + epsilon)
    normed = (hidden_float * inv_in * full_gain.astype(jnp.float32)[None, :]).astype(jnp.bfloat16)
    gate_in = jnp.dot(normed, gate_all, preferred_element_type=jnp.float32)
    inner_in = jnp.dot(normed, inner_all, preferred_element_type=jnp.float32)
    state_in = jnp.dot(normed, states_all, preferred_element_type=jnp.float32)
    step_in = jnp.dot(normed, step_all, preferred_element_type=jnp.float32)
    near_masks = shift_masks(doc_row)
    mixer_local = partial(mixer_core, near_masks, doc_row)
    gated_vals, core_back = jax.vjp(
        mixer_local,
        gate_in,
        inner_in,
        state_in,
        step_in,
        conv_inner_weight,
        conv_inner_bias,
        conv_state_weight,
        conv_state_bias,
        step_bias,
        decay_log,
        skip_gain,
    )
    inner_width = gated_vals.shape[1] * lax.axis_size("col")
    gated_sq = lax.psum(jnp.sum(gated_vals * gated_vals, axis=1), "col")
    inv_gated = lax.rsqrt(gated_sq / inner_width + epsilon)[:, None]
    hat_gated = gated_vals * inv_gated
    normed_out = (hat_gated * gated_gain[None, :]).astype(jnp.bfloat16)
    out_part = jnp.dot(normed_out, out_all, preferred_element_type=jnp.float32)
    out_share = lax.psum_scatter(out_part, "col", scatter_dimension=1, tiled=True)
    block_out = (hidden_in.astype(jnp.float32) + out_share).astype(jnp.bfloat16)
    grad_out_full = jnp.einsum(
        "ti,td->id", normed_out, full_grad, preferred_element_type=jnp.float32
    )
    grad_normed_out = jnp.einsum(
        "td,id->ti", full_grad, out_all, preferred_element_type=jnp.float32
    )
    scaled_out = grad_normed_out * gated_gain[None, :]
    grad_gated_gain = jnp.sum(grad_normed_out * hat_gated, axis=0)
    dot_gated = lax.psum(jnp.sum(scaled_out * hat_gated, axis=1), "col")
    grad_gated = inv_gated * (scaled_out - hat_gated * (dot_gated / inner_width)[:, None])
    (
        grad_gate,
        grad_inner,
        grad_state,
        grad_step,
        grad_conv_inner_weight,
        grad_conv_inner_bias,
        grad_conv_state_weight,
        grad_conv_state_bias,
        grad_step_bias,
        grad_decay_log,
        grad_skip_gain,
    ) = core_back(grad_gated)
    gate_back = grad_gate.astype(jnp.bfloat16)
    inner_back = grad_inner.astype(jnp.bfloat16)
    step_back = grad_step.astype(jnp.bfloat16)
    grad_gate_full = jnp.einsum("td,tf->df", normed, gate_back, preferred_element_type=jnp.float32)
    grad_inner_full = jnp.einsum(
        "td,tf->df", normed, inner_back, preferred_element_type=jnp.float32
    )
    grad_step_full = jnp.einsum("td,tf->df", normed, step_back, preferred_element_type=jnp.float32)
    grad_states_full = jnp.einsum(
        "td,tf->df", normed.astype(jnp.float32), grad_state, precision=highest
    )
    grad_normed = jnp.einsum("tf,df->td", gate_back, gate_all, preferred_element_type=jnp.float32)
    grad_normed = grad_normed + jnp.einsum(
        "tf,df->td", inner_back, inner_all, preferred_element_type=jnp.float32
    )
    grad_normed = grad_normed + jnp.einsum(
        "tf,df->td", step_back, step_all, preferred_element_type=jnp.float32
    )
    grad_normed = grad_normed + jnp.einsum(
        "tf,df->td", grad_state, states_all.astype(jnp.float32), precision=highest
    )
    grad_share = lax.psum_scatter(grad_normed, "col", scatter_dimension=1, tiled=True)
    hat_own = hidden_in.astype(jnp.float32) * inv_in
    scaled_in = grad_share * norm_gain.astype(jnp.float32)[None, :]
    grad_norm_gain = jnp.sum(grad_share * hat_own, axis=0)
    dot_in, grad_states_full, grad_conv_state_weight, grad_conv_state_bias = lax.psum(
        (
            jnp.sum(scaled_in * hat_own, axis=1),
            grad_states_full,
            grad_conv_state_weight,
            grad_conv_state_bias,
        ),
        "col",
    )
    grad_hidden = out_grad.astype(jnp.float32) + inv_in * (
        scaled_in - hat_own * (dot_in / model_width)[:, None]
    )
    rows_per = proj_gate.shape[0]
    cols_per = proj_out.shape[1]
    summed = lax.psum(
        (
            grad_gate_full,
            grad_inner_full,
            grad_states_full,
            grad_step_full,
            grad_out_full,
            grad_norm_gain,
            grad_conv_inner_weight,
            grad_conv_inner_bias,
            grad_conv_state_weight,
            grad_conv_state_bias,
            grad_step_bias,
            grad_decay_log,
            grad_skip_gain,
            grad_gated_gain,
        ),
        ("dp", "row"),
    )
    row_place = lax.axis_index("row")
    grad_proj_gate = lax.dynamic_slice_in_dim(summed[0], row_place * rows_per, rows_per, 0)
    grad_proj_inner = lax.dynamic_slice_in_dim(summed[1], row_place * rows_per, rows_per, 0)
    grad_proj_states = lax.dynamic_slice_in_dim(summed[2], row_place * rows_per, rows_per, 0)
    grad_proj_step = lax.dynamic_slice_in_dim(summed[3], row_place * rows_per, rows_per, 0)
    grad_proj_out = lax.dynamic_slice_in_dim(summed[4], row_place * cols_per, cols_per, 1)
    smalls = summed[5:]
    return (
        block_out,
        grad_hidden,
        smalls[0],
        grad_proj_gate,
        grad_proj_inner,
        grad_proj_states,
        grad_proj_step,
        smalls[1],
        smalls[2],
        smalls[3],
        smalls[4],
        smalls[5],
        smalls[6],
        smalls[7],
        smalls[8],
        grad_proj_out,
    )


def solution(mesh):
    in_specs = (
        P(("dp", "row"), "col"),
        P(("dp", "row"), None),
        P("col"),
        P("row", "col"),
        P("row", "col"),
        P("row", None),
        P("row", "col"),
        P(None, "col"),
        P("col"),
        P(),
        P(),
        P("col"),
        P("col"),
        P("col"),
        P("col"),
        P("col", "row"),
        P(("dp", "row"), "col"),
    )
    out_specs = (
        P(("dp", "row"), "col"),
        P(("dp", "row"), "col"),
        P("col"),
        P("row", "col"),
        P("row", "col"),
        P("row", None),
        P("row", "col"),
        P(None, "col"),
        P("col"),
        P(),
        P(),
        P("col"),
        P("col"),
        P("col"),
        P("col"),
        P("col", "row"),
    )
    return jax.shard_map(body, mesh=mesh, in_specs=in_specs, out_specs=out_specs, check_vma=False)
```

profile of v0, /device:TPU:0, one launch (start us, length us, event | category | flops | bytes accessed | tf_op | source)
XLA Modules:
  0.0 1338.9 jit_solution(13862099299180901162)
XLA Ops:
  13.4 11.6 all_gather.28
  26.1 8.1 all-gather.1
  48.2 6.8 all-gather.10.cloned.1.call-done
  59.1 8.7 subtract_add_fusion
  67.8 6.6 copy.122
  74.4 6.0 copy.194
  90.7 283.6 %while.47 = (s32[]{:T(128)}, f32[12,64,128]{2,1,0:T(8,128)S(1)}, s32[]{:T(128)}, f32[8,256,12,64]{1,0,3,2:T(8,128)}, f32[8,12,64,128]{3,2,1,0:T(8,128)}, /*index...) while((s32[]{:T(128)}, f32[12,64,128]{2,1,0:T(8,128)S(1)}, ...), condition=%wide.region_4.5_spmd.clone, body=%wide.region_1.4_spmd.clone.sunk | while | flops 660386880 | bytes 11892011 | solution.py:94
  103.1 18.5 %dynamic_update_slice.87 = f32[8,256,12,64]{1,0,3,2:T(8,128)} dynamic-update-slice(f32[8,256,12,64]{1,0,3,2:T(8,128)} %get-tuple-element.1230, f32[1,256,12,64]{1,0,3,2:T(1,128)S(1)} %copy.223, s32[]{:T(128)} %get-tuple-element.1227, s32[]{:T(128)} %constant.139.clone.1..sunk, s32[]{:T(128)} %constant.139.clone.1..sunk, s32[]{:T(128)} %constant.139.clone.1..sunk) | dynamic-update-slice | bytes 1572868 | tf_op jit(solution)/shard_map/jvp()/while/body/jit(dynamic_update_index_in_dim)/dynamic_update_slice | solution.py:94
  138.7 18.5 %dynamic_update_slice.87 = f32[8,256,12,64]{1,0,3,2:T(8,128)} dynamic-update-slice(f32[8,256,12,64]{1,0,3,2:T(8,128)} %get-tuple-element.1230, f32[1,256,12,64]{1,0,3,2:T(1,128)S(1)} %copy.223, s32[]{:T(128)} %get-tuple-element.1227, s32[]{:T(128)} %constant.139.clone.1..sunk, s32[]{:T(128)} %constant.139.clone.1..sunk, s32[]{:T(128)} %constant.139.clone.1..sunk) | dynamic-update-slice | bytes 1572868 | tf_op jit(solution)/shard_map/jvp()/while/body/jit(dynamic_update_index_in_dim)/dynamic_update_slice | solution.py:94
  174.0 18.5 %dynamic_update_slice.87 = f32[8,256,12,64]{1,0,3,2:T(8,128)} dynamic-update-slice(f32[8,256,12,64]{1,0,3,2:T(8,128)} %get-tuple-element.1230, f32[1,256,12,64]{1,0,3,2:T(1,128)S(1)} %copy.223, s32[]{:T(128)} %get-tuple-element.1227, s32[]{:T(128)} %constant.139.clone.1..sunk, s32[]{:T(128)} %constant.139.clone.1..sunk, s32[]{:T(128)} %constant.139.clone.1..sunk) | dynamic-update-slice | bytes 1572868 | tf_op jit(solution)/shard_map/jvp()/while/body/jit(dynamic_update_index_in_dim)/dynamic_update_slice | solution.py:94
  209.4 18.5 %dynamic_update_slice.87 = f32[8,256,12,64]{1,0,3,2:T(8,128)} dynamic-update-slice(f32[8,256,12,64]{1,0,3,2:T(8,128)} %get-tuple-element.1230, f32[1,256,12,64]{1,0,3,2:T(1,128)S(1)} %copy.223, s32[]{:T(128)} %get-tuple-element.1227, s32[]{:T(128)} %constant.139.clone.1..sunk, s32[]{:T(128)} %constant.139.clone.1..sunk, s32[]{:T(128)} %constant.139.clone.1..sunk) | dynamic-update-slice | bytes 1572868 | tf_op jit(solution)/shard_map/jvp()/while/body/jit(dynamic_update_index_in_dim)/dynamic_update_slice | solution.py:94
  244.8 18.5 %dynamic_update_slice.87 = f32[8,256,12,64]{1,0,3,2:T(8,128)} dynamic-update-slice(f32[8,256,12,64]{1,0,3,2:T(8,128)} %get-tuple-element.1230, f32[1,256,12,64]{1,0,3,2:T(1,128)S(1)} %copy.223, s32[]{:T(128)} %get-tuple-element.1227, s32[]{:T(128)} %constant.139.clone.1..sunk, s32[]{:T(128)} %constant.139.clone.1..sunk, s32[]{:T(128)} %constant.139.clone.1..sunk) | dynamic-update-slice | bytes 1572868 | tf_op jit(solution)/shard_map/jvp()/while/body/jit(dynamic_update_index_in_dim)/dynamic_update_slice | solution.py:94
  280.1 18.5 %dynamic_update_slice.87 = f32[8,256,12,64]{1,0,3,2:T(8,128)} dynamic-update-slice(f32[8,256,12,64]{1,0,3,2:T(8,128)} %get-tuple-element.1230, f32[1,256,12,64]{1,0,3,2:T(1,128)S(1)} %copy.223, s32[]{:T(128)} %get-tuple-element.1227, s32[]{:T(128)} %constant.139.clone.1..sunk, s32[]{:T(128)} %constant.139.clone.1..sunk, s32[]{:T(128)} %constant.139.clone.1..sunk) | dynamic-update-slice | bytes 1572868 | tf_op jit(solution)/shard_map/jvp()/while/body/jit(dynamic_update_index_in_dim)/dynamic_update_slice | solution.py:94
  315.5 18.5 %dynamic_update_slice.87 = f32[8,256,12,64]{1,0,3,2:T(8,128)} dynamic-update-slice(f32[8,256,12,64]{1,0,3,2:T(8,128)} %get-tuple-element.1230, f32[1,256,12,64]{1,0,3,2:T(1,128)S(1)} %copy.223, s32[]{:T(128)} %get-tuple-element.1227, s32[]{:T(128)} %constant.139.clone.1..sunk, s32[]{:T(128)} %constant.139.clone.1..sunk, s32[]{:T(128)} %constant.139.clone.1..sunk) | dynamic-update-slice | bytes 1572868 | tf_op jit(solution)/shard_map/jvp()/while/body/jit(dynamic_update_index_in_dim)/dynamic_update_slice | solution.py:94
  350.9 18.5 %dynamic_update_slice.87 = f32[8,256,12,64]{1,0,3,2:T(8,128)} dynamic-update-slice(f32[8,256,12,64]{1,0,3,2:T(8,128)} %get-tuple-element.1230, f32[1,256,12,64]{1,0,3,2:T(1,128)S(1)} %copy.223, s32[]{:T(128)} %get-tuple-element.1227, s32[]{:T(128)} %constant.139.clone.1..sunk, s32[]{:T(128)} %constant.139.clone.1..sunk, s32[]{:T(128)} %constant.139.clone.1..sunk) | dynamic-update-slice | bytes 1572868 | tf_op jit(solution)/shard_map/jvp()/while/body/jit(dynamic_update_index_in_dim)/dynamic_update_slice | solution.py:94
  374.3 8.5 copy.195
  382.9 6.8 copy.127
  389.6 8.4 multiply_reduce_fusion.11
  400.8 10.5 multiply_reduce_fusion.5
  413.7 13.8 %fusion.100 = (bf16[2048,768]{1,0:T(8,128)(2,1)}, f32[2048,768]{1,0:T(8,128)}) fusion(f32[2048,768]{1,0:T(8,128)} %get-tuple-element.935, f32[2048,768]{1,0:T(8,128)} %copy.127, f32[2048]{0:T(1024)S(1)} %broadcast_multiply_fusion.7, f32[2048,768]{1,0:T(8,128)} %get-tuple-element.889, f32[2048,768]{1,0:T(8,128)} %get-tuple-element.936, ...), kind=kLoop, calls=%fused_computation.154 | loop fusion | flops 28311552 | bytes 34622464 | tf_op jit(solution)/shard_map/convert_element_type | solution.py:219
  427.5 6.6 copy.130
  434.1 8.5 copy.196
  449.4 434.8 %while.48 = (s32[]{:T(128)}, f32[12]{0:T(128)}, f32[12,64,128]{2,1,0:T(8,128)S(1)}, f32[8,256,12,64]{1,0,3,2:T(8,128)}, f32[8,256,128]{2,1,0:T(8,128)}, /*index=...) while((s32[]{:T(128)}, f32[12]{0:T(128)}, ...), condition=%wide.region_23.24_spmd.clone, body=%wide.region_10.23_spmd.clone.sunk | while | flops 1529836544 | bytes 32442236 | solution.py:94
  480.7 18.5 %dynamic_update_slice.93 = f32[8,256,12,64]{1,0,3,2:T(8,128)} dynamic-update-slice(f32[8,256,12,64]{1,0,3,2:T(8,128)} %get-tuple-element.1286, f32[1,256,12,64]{1,0,3,2:T(1,128)S(1)} %copy.230, s32[]{:T(128)S(6)} %sub.308, s32[]{:T(128)} %constant.139.clone.1..sunk.1, s32[]{:T(128)} %constant.139.clone.1..sunk.1, s32[]{:T(128)} %constant.139.clone.1..sunk.1) | dynamic-update-slice | bytes 1572868 | tf_op jit(solution)/shard_map/transpose(jvp())/while/body/jit(dynamic_update_index_in_dim)/dynamic_update_slice | solution.py:94
  535.0 18.5 %dynamic_update_slice.93 = f32[8,256,12,64]{1,0,3,2:T(8,128)} dynamic-update-slice(f32[8,256,12,64]{1,0,3,2:T(8,128)} %get-tuple-element.1286, f32[1,256,12,64]{1,0,3,2:T(1,128)S(1)} %copy.230, s32[]{:T(128)S(6)} %sub.308, s32[]{:T(128)} %constant.139.clone.1..sunk.1, s32[]{:T(128)} %constant.139.clone.1..sunk.1, s32[]{:T(128)} %constant.139.clone.1..sunk.1) | dynamic-update-slice | bytes 1572868 | tf_op jit(solution)/shard_map/transpose(jvp())/while/body/jit(dynamic_update_index_in_dim)/dynamic_update_slice | solution.py:94
  589.3 18.5 %dynamic_update_slice.93 = f32[8,256,12,64]{1,0,3,2:T(8,128)} dynamic-update-slice(f32[8,256,12,64]{1,0,3,2:T(8,128)} %get-tuple-element.1286, f32[1,256,12,64]{1,0,3,2:T(1,128)S(1)} %copy.230, s32[]{:T(128)S(6)} %sub.308, s32[]{:T(128)} %constant.139.clone.1..sunk.1, s32[]{:T(128)} %constant.139.clone.1..sunk.1, s32[]{:T(128)} %constant.139.clone.1..sunk.1) | dynamic-update-slice | bytes 1572868 | tf_op jit(solution)/shard_map/transpose(jvp())/while/body/jit(dynamic_update_index_in_dim)/dynamic_update_slice | solution.py:94
  643.6 18.5 %dynamic_update_slice.93 = f32[8,256,12,64]{1,0,3,2:T(8,128)} dynamic-update-slice(f32[8,256,12,64]{1,0,3,2:T(8,128)} %get-tuple-element.1286, f32[1,256,12,64]{1,0,3,2:T(1,128)S(1)} %copy.230, s32[]{:T(128)S(6)} %sub.308, s32[]{:T(128)} %constant.139.clone.1..sunk.1, s32[]{:T(128)} %constant.139.clone.1..sunk.1, s32[]{:T(128)} %constant.139.clone.1..sunk.1) | dynamic-update-slice | bytes 1572868 | tf_op jit(solution)/shard_map/transpose(jvp())/while/body/jit(dynamic_update_index_in_dim)/dynamic_update_slice | solution.py:94
  697.8 18.5 %dynamic_update_slice.93 = f32[8,256,12,64]{1,0,3,2:T(8,128)} dynamic-update-slice(f32[8,256,12,64]{1,0,3,2:T(8,128)} %get-tuple-element.1286, f32[1,256,12,64]{1,0,3,2:T(1,128)S(1)} %copy.230, s32[]{:T(128)S(6)} %sub.308, s32[]{:T(128)} %constant.139.clone.1..sunk.1, s32[]{:T(128)} %constant.139.clone.1..sunk.1, s32[]{:T(128)} %constant.139.clone.1..sunk.1) | dynamic-update-slice | bytes 1572868 | tf_op jit(solution)/shard_map/transpose(jvp())/while/body/jit(dynamic_update_index_in_dim)/dynamic_update_slice | solution.py:94
  752.1 18.5 %dynamic_update_slice.93 = f32[8,256,12,64]{1,0,3,2:T(8,128)} dynamic-update-slice(f32[8,256,12,64]{1,0,3,2:T(8,128)} %get-tuple-element.1286, f32[1,256,12,64]{1,0,3,2:T(1,128)S(1)} %copy.230, s32[]{:T(128)S(6)} %sub.308, s32[]{:T(128)} %constant.139.clone.1..sunk.1, s32[]{:T(128)} %constant.139.clone.1..sunk.1, s32[]{:T(128)} %constant.139.clone.1..sunk.1) | dynamic-update-slice | bytes 1572868 | tf_op jit(solution)/shard_map/transpose(jvp())/while/body/jit(dynamic_update_index_in_dim)/dynamic_update_slice | solution.py:94
  806.4 18.5 %dynamic_update_slice.93 = f32[8,256,12,64]{1,0,3,2:T(8,128)} dynamic-update-slice(f32[8,256,12,64]{1,0,3,2:T(8,128)} %get-tuple-element.1286, f32[1,256,12,64]{1,0,3,2:T(1,128)S(1)} %copy.230, s32[]{:T(128)S(6)} %sub.308, s32[]{:T(128)} %constant.139.clone.1..sunk.1, s32[]{:T(128)} %constant.139.clone.1..sunk.1, s32[]{:T(128)} %constant.139.clone.1..sunk.1) | dynamic-update-slice | bytes 1572868 | tf_op jit(solution)/shard_map/transpose(jvp())/while/body/jit(dynamic_update_index_in_dim)/dynamic_update_slice | solution.py:94
  860.6 18.5 %dynamic_update_slice.93 = f32[8,256,12,64]{1,0,3,2:T(8,128)} dynamic-update-slice(f32[8,256,12,64]{1,0,3,2:T(8,128)} %get-tuple-element.1286, f32[1,256,12,64]{1,0,3,2:T(1,128)S(1)} %copy.230, s32[]{:T(128)S(6)} %sub.308, s32[]{:T(128)} %constant.139.clone.1..sunk.1, s32[]{:T(128)} %constant.139.clone.1..sunk.1, s32[]{:T(128)} %constant.139.clone.1..sunk.1) | dynamic-update-slice | bytes 1572868 | tf_op jit(solution)/shard_map/transpose(jvp())/while/body/jit(dynamic_update_index_in_dim)/dynamic_update_slice | solution.py:94
  884.2 8.5 copy.197
  892.7 6.7 copy.134
  899.4 8.4 multiply_reduce_fusion.9
  907.9 6.4 multiply_reduce_fusion.8
  914.3 6.2 slice_multiply_fusion.1
  926.9 10.2 fusion.130
  937.2 6.2 fusion.147
  951.2 4.5 fusion.148
  955.9 6.1 fusion.146
  962.0 7.3 fusion.128
  969.3 5.7 all-reduce.32.cloned.1.call-done
  979.0 4.7 fusion.145
  993.5 8.4 fusion.129
  1003.4 223.1 %all-reduce.34.cloned.1.call-done = (f32[768,768]{1,0:T(8,128)}, f32[768,768]{1,0:T(8,128)}, f32[768,256]{1,0:T(8,128)}, f32[768,768]{0,1:T(8,128)}) async-done(((f32[768,768]{1,0:T(8,128)}, f32[768,768]{1,0:T(8,128)}, f32[768,256]{1,0:T(8,128)}, f32[768,768]{0,1:T(8,128)}), (f32[768,768]{1,0:T(8,128)}, f32[768,768]{1,0:T(8,128)}, f32[768,256]{1,0:T(8,128)}, ...) | async-done | bytes 7864336 | tf_op jit(solution)/shard_map/psum | solution.py:258
  1234.1 7.7 reduce-scatter.5.cloned.1.call-done
  1248.1 78.5 %all-reduce.26 = (f32[384]{0:T(512)}, f32[768,12]{0,1:T(8,128)S(1)}, f32[4,768]{1,0:T(4,128)}, f32[768]{0:T(1024)}, f32[4,256]{1,0:T(4,128)}, /*index=5*/f32[256...) all-reduce(f32[384]{0:T(512)S(1)} %get-tuple-element.779, ...), channel_id=1, replica_groups=mesh['dp'=4,'row'=4,'col'=2] {'dp','row'}, use_global_device_ids=true, to_apply=%region_28.29 | all-reduce | flops 15524 | bytes 124192 | tf_op jit(solution)/shard_map/psum | solution.py:258
  1327.4 4.8 fusion.111
  (1033 shorter events, 488.8 us)
Async XLA Ops:
  7.2 17.7 %copy-start.82 = (f32[4,256]{1,0:T(4,128)S(1)}, f32[4,256]{1,0:T(4,128)}, u32[]{:S(2)}) copy-start(f32[4,256]{1,0:T(4,128)} %param.30) | copy-start | bytes 12292
  7.2 18.3 %copy-start.59 = (f32[4,768]{1,0:T(4,128)S(1)}, f32[4,768]{1,0:T(4,128)}, u32[]{:S(2)}) copy-start(f32[4,768]{1,0:T(4,128)} %param.28) | copy-start | bytes 36868
  7.2 18.9 %copy-start.68 = (bf16[192,12]{0,1:T(8,128)(2,1)S(1)}, bf16[192,12]{0,1:T(8,128)(2,1)}, u32[]{:S(2)}) copy-start(bf16[192,12]{0,1:T(8,128)(2,1)} %param.27) | copy-start | bytes 13828
  7.2 27.7 %copy-start.90 = (f32[12]{0:T(128)S(1)}, f32[12]{0:T(128)}, u32[]{:S(2)}) copy-start(f32[12]{0:T(128)} %param.33) | copy-start | bytes 148
  7.2 28.8 %copy-start.30 = (s32[1,2048]{1,0:T(1,128)S(1)}, s32[1,2048]{1,0:T(1,128)}, u32[]{:S(2)}) copy-start(s32[1,2048]{1,0:T(1,128)} %param.22) | copy-start | bytes 24580
  7.3 30.7 %all-gather.8.cloned.1.call-start = ((), (), s32[]{:S(2)}) async-start(), calls=%async_computation.2 | async-start | bytes 4718592 | tf_op jit(solution)/shard_map/all_gather | solution.py:153
  8.0 47.0 %all-gather.10.cloned.1.call-start = ((), (), s32[]{:S(2)}) async-start(), calls=%async_computation.3 | async-start | bytes 1474560 | tf_op jit(solution)/shard_map/all_gather | solution.py:159
  8.7 380.9 %all-gather.12.cloned.1.call-start = ((), (), s32[]{:S(2)}) async-start(), calls=%async_computation.4 | async-start | bytes 1474560 | tf_op jit(solution)/shard_map/all_gather | solution.py:158
  9.5 391.3 %all-gather.14.cloned.1.call-start = ((), (), s32[]{:S(2)}) async-start(), calls=%async_computation.5 | async-start | bytes 1474560 | tf_op jit(solution)/shard_map/all_gather | solution.py:162
  10.1 390.7 %all-gather.16.cloned.1.call-start = ((), (), s32[]{:S(2)}) async-start(), calls=%async_computation.7 | async-start | bytes 4718592 | tf_op jit(solution)/shard_map/all_gather | solution.py:154
  10.6 964.3 %all-reduce.32.cloned.1.call-start = ((), (), s32[]{:S(2)}) async-start(), calls=%async_computation.9 | async-start | bytes 1572864 | tf_op jit(solution)/shard_map/psum | solution.py:244
  38.0 21.1 %copy-start.31 = (f32[2048]{0:T(1024)}, f32[2048]{0:T(1024)S(1)}, u32[]{:S(2)}) copy-start(f32[2048]{0:T(1024)S(1)} %get-tuple-element.928) | copy-start | bytes 24580
  38.0 21.1 %copy-start.33 = (f32[2048]{0:T(1024)}, f32[2048]{0:T(1024)S(1)}, u32[]{:S(2)}) copy-start(f32[2048]{0:T(1024)S(1)} %get-tuple-element.927) | copy-start | bytes 24580
  41.9 43.2 %copy-start.3 = (bf16[2048,768]{1,0:T(8,128)(2,1)}, bf16[2048,768]{1,0:T(8,128)(2,1)S(1)}, u32[]{:S(2)}) copy-start(bf16[2048,768]{1,0:T(8,128)(2,1)S(1)} %fusion.97) | copy-start | bytes 9437188
  479.9 22.8 %copy-start.29 = (f32[12]{0:T(128)S(1)}, f32[12]{0:T(128)}, u32[]{:S(2)}) copy-start(f32[12]{0:T(128)} %copy-done.28) | copy-start | bytes 148 | tf_op jit(solution)/shard_map/transpose(jvp())/while
  479.9 23.5 %copy-start.51 = (f32[12]{0:T(128)S(1)}, f32[12]{0:T(128)}, u32[]{:S(2)}) copy-start(f32[12]{0:T(128)} %get-tuple-element.1284) | copy-start | bytes 148 | tf_op jit(solution)/shard_map/transpose(jvp())/while
  479.9 24.0 %copy-start.22 = (f32[8,12,256]{2,1,0:T(8,128)S(1)}, f32[8,12,256]{2,1,0:T(8,128)}, u32[]{:S(2)}) copy-start(f32[8,12,256]{2,1,0:T(8,128)} %copy-done.21) | copy-start | bytes 294916 | tf_op jit(solution)/shard_map/transpose(jvp())/while
  534.2 22.8 %copy-start.29 = (f32[12]{0:T(128)S(1)}, f32[12]{0:T(128)}, u32[]{:S(2)}) copy-start(f32[12]{0:T(128)} %copy-done.28) | copy-start | bytes 148 | tf_op jit(solution)/shard_map/transpose(jvp())/while
  534.2 23.5 %copy-start.51 = (f32[12]{0:T(128)S(1)}, f32[12]{0:T(128)}, u32[]{:S(2)}) copy-start(f32[12]{0:T(128)} %get-tuple-element.1284) | copy-start | bytes 148 | tf_op jit(solution)/shard_map/transpose(jvp())/while
  534.2 24.0 %copy-start.22 = (f32[8,12,256]{2,1,0:T(8,128)S(1)}, f32[8,12,256]{2,1,0:T(8,128)}, u32[]{:S(2)}) copy-start(f32[8,12,256]{2,1,0:T(8,128)} %copy-done.21) | copy-start | bytes 294916 | tf_op jit(solution)/shard_map/transpose(jvp())/while
  588.4 22.8 %copy-start.29 = (f32[12]{0:T(128)S(1)}, f32[12]{0:T(128)}, u32[]{:S(2)}) copy-start(f32[12]{0:T(128)} %copy-done.28) | copy-start | bytes 148 | tf_op jit(solution)/shard_map/transpose(jvp())/while
  588.4 23.5 %copy-start.51 = (f32[12]{0:T(128)S(1)}, f32[12]{0:T(128)}, u32[]{:S(2)}) copy-start(f32[12]{0:T(128)} %get-tuple-element.1284) | copy-start | bytes 148 | tf_op jit(solution)/shard_map/transpose(jvp())/while
  588.5 24.0 %copy-start.22 = (f32[8,12,256]{2,1,0:T(8,128)S(1)}, f32[8,12,256]{2,1,0:T(8,128)}, u32[]{:S(2)}) copy-start(f32[8,12,256]{2,1,0:T(8,128)} %copy-done.21) | copy-start | bytes 294916 | tf_op jit(solution)/shard_map/transpose(jvp())/while
  642.7 22.8 %copy-start.29 = (f32[12]{0:T(128)S(1)}, f32[12]{0:T(128)}, u32[]{:S(2)}) copy-start(f32[12]{0:T(128)} %copy-done.28) | copy-start | bytes 148 | tf_op jit(solution)/shard_map/transpose(jvp())/while
  642.7 23.5 %copy-start.51 = (f32[12]{0:T(128)S(1)}, f32[12]{0:T(128)}, u32[]{:S(2)}) copy-start(f32[12]{0:T(128)} %get-tuple-element.1284) | copy-start | bytes 148 | tf_op jit(solution)/shard_map/transpose(jvp())/while
  642.7 24.0 %copy-start.22 = (f32[8,12,256]{2,1,0:T(8,128)S(1)}, f32[8,12,256]{2,1,0:T(8,128)}, u32[]{:S(2)}) copy-start(f32[8,12,256]{2,1,0:T(8,128)} %copy-done.21) | copy-start | bytes 294916 | tf_op jit(solution)/shard_map/transpose(jvp())/while
  697.0 22.8 %copy-start.29 = (f32[12]{0:T(128)S(1)}, f32[12]{0:T(128)}, u32[]{:S(2)}) copy-start(f32[12]{0:T(128)} %copy-done.28) | copy-start | bytes 148 | tf_op jit(solution)/shard_map/transpose(jvp())/while
  697.0 23.5 %copy-start.51 = (f32[12]{0:T(128)S(1)}, f32[12]{0:T(128)}, u32[]{:S(2)}) copy-start(f32[12]{0:T(128)} %get-tuple-element.1284) | copy-start | bytes 148 | tf_op jit(solution)/shard_map/transpose(jvp())/while
  697.0 24.0 %copy-start.22 = (f32[8,12,256]{2,1,0:T(8,128)S(1)}, f32[8,12,256]{2,1,0:T(8,128)}, u32[]{:S(2)}) copy-start(f32[8,12,256]{2,1,0:T(8,128)} %copy-done.21) | copy-start | bytes 294916 | tf_op jit(solution)/shard_map/transpose(jvp())/while
  751.2 22.8 %copy-start.29 = (f32[12]{0:T(128)S(1)}, f32[12]{0:T(128)}, u32[]{:S(2)}) copy-start(f32[12]{0:T(128)} %copy-done.28) | copy-start | bytes 148 | tf_op jit(solution)/shard_map/transpose(jvp())/while
  751.2 23.5 %copy-start.51 = (f32[12]{0:T(128)S(1)}, f32[12]{0:T(128)}, u32[]{:S(2)}) copy-start(f32[12]{0:T(128)} %get-tuple-element.1284) | copy-start | bytes 148 | tf_op jit(solution)/shard_map/transpose(jvp())/while
  751.3 24.0 %copy-start.22 = (f32[8,12,256]{2,1,0:T(8,128)S(1)}, f32[8,12,256]{2,1,0:T(8,128)}, u32[]{:S(2)}) copy-start(f32[8,12,256]{2,1,0:T(8,128)} %copy-done.21) | copy-start | bytes 294916 | tf_op jit(solution)/shard_map/transpose(jvp())/while
  805.5 22.8 %copy-start.29 = (f32[12]{0:T(128)S(1)}, f32[12]{0:T(128)}, u32[]{:S(2)}) copy-start(f32[12]{0:T(128)} %copy-done.28) | copy-start | bytes 148 | tf_op jit(solution)/shard_map/transpose(jvp())/while
  805.5 23.5 %copy-start.51 = (f32[12]{0:T(128)S(1)}, f32[12]{0:T(128)}, u32[]{:S(2)}) copy-start(f32[12]{0:T(128)} %get-tuple-element.1284) | copy-start | bytes 148 | tf_op jit(solution)/shard_map/transpose(jvp())/while
  805.5 24.0 %copy-start.22 = (f32[8,12,256]{2,1,0:T(8,128)S(1)}, f32[8,12,256]{2,1,0:T(8,128)}, u32[]{:S(2)}) copy-start(f32[8,12,256]{2,1,0:T(8,128)} %copy-done.21) | copy-start | bytes 294916 | tf_op jit(solution)/shard_map/transpose(jvp())/while
  859.8 22.8 %copy-start.29 = (f32[12]{0:T(128)S(1)}, f32[12]{0:T(128)}, u32[]{:S(2)}) copy-start(f32[12]{0:T(128)} %copy-done.28) | copy-start | bytes 148 | tf_op jit(solution)/shard_map/transpose(jvp())/while
  859.8 23.5 %copy-start.51 = (f32[12]{0:T(128)S(1)}, f32[12]{0:T(128)}, u32[]{:S(2)}) copy-start(f32[12]{0:T(128)} %get-tuple-element.1284) | copy-start | bytes 148 | tf_op jit(solution)/shard_map/transpose(jvp())/while
  859.8 24.0 %copy-start.22 = (f32[8,12,256]{2,1,0:T(8,128)S(1)}, f32[8,12,256]{2,1,0:T(8,128)}, u32[]{:S(2)}) copy-start(f32[8,12,256]{2,1,0:T(8,128)} %copy-done.21) | copy-start | bytes 294916 | tf_op jit(solution)/shard_map/transpose(jvp())/while
  892.7 15.2 %slice-start = ((s8[6291456]{0:T(1024)(128)(4,1)}), s8[2097152]{0:T(1024)(128)(4,1)S(1)}, s32[]{:S(2)}) async-start(s8[6291456]{0:T(1024)(128)(4,1)} %bitcast.356), calls=%async_computation.11 | async-start | bytes 4194304
  955.8 270.8 %all-reduce.34.cloned.1.call-start = ((), (), s32[]{:S(2)}) async-start(), calls=%async_computation.10 | async-start | bytes 15728640 | tf_op jit(solution)/shard_map/psum | solution.py:258
  975.0 266.8 %reduce-scatter.5.cloned.1.call-start = ((), (), s32[]{:S(2)}) async-start(), calls=%async_computation.8 | async-start | bytes 9437184 | tf_op jit(solution)/shard_map/reduce_scatter | solution.py:240
  992.9 334.5 %reduce-scatter.3.cloned.1.call-start = ((), (), s32[]{:S(2)}) async-start(), calls=%async_computation.6 | async-start | bytes 9437184 | tf_op jit(solution)/shard_map/reduce_scatter | solution.py:194
  1002.9 238.8 %copy-start.39 = (f32[2048]{0:T(1024)S(1)}, f32[2048]{0:T(1024)}, u32[]{:S(2)}) copy-start(f32[2048]{0:T(1024)} %copy-done.38) | copy-start | bytes 24580
  1003.4 238.3 %copy-start.10 = (bf16[2048,384]{1,0:T(8,128)(2,1)S(1)}, bf16[2048,384]{1,0:T(8,128)(2,1)}, u32[]{:S(2)}) copy-start(bf16[2048,384]{1,0:T(8,128)(2,1)} %param.21) | copy-start | bytes 4718596
  1232.0 16.1 %copy-start.53 = (f32[12]{0:T(128)S(1)}, f32[12]{0:T(128)}, u32[]{:S(2)}) copy-start(f32[12]{0:T(128)} %get-tuple-element.531) | copy-start | bytes 148
  1232.0 16.1 %copy-start.79 = (f32[768]{0:T(1024)S(1)}, f32[768]{0:T(1024)}, u32[]{:S(2)}) copy-start(f32[768]{0:T(1024)} %get-tuple-element.775) | copy-start | bytes 9220
  1232.0 16.1 %copy-start.83 = (f32[12]{0:T(128)S(1)}, f32[12]{0:T(128)}, u32[]{:S(2)}) copy-start(f32[12]{0:T(128)} %get-tuple-element.872) | copy-start | bytes 148
  1232.0 95.3 %copy-start.14 = (bf16[2048,384]{1,0:T(8,128)(2,1)S(1)}, bf16[2048,384]{1,0:T(8,128)(2,1)}, u32[]{:S(2)}) copy-start(bf16[2048,384]{1,0:T(8,128)(2,1)} %param.37) | copy-start | bytes 4718596
  (111 other events, 531.8 us)
Sparse Core Ops, SparseCore 0:
  9.6 14.7 all-gather.7
  26.2 28.7 all-gather.9
  56.9 27.5 all-gather.11
  86.2 27.6 all-gather.13
  115.2 12.0 all-gather.15
  955.9 18.9 all-reduce.31
  981.4 245.1 all-reduce.33
  1228.8 12.8 reduce-scatter.4
  1244.0 15.1 reduce-scatter.2
where the time goes:
time: 1350 us; the launch traced here: 1340 us
  local copies, waits for them, and re-layouts  528 us (39%)
  waiting for transfers between devices  247 us (18%)
  matrix products  241 us (18%)
  other arithmetic  174 us (13%)
  blocking collectives  109 us (8%)
  loops' own time  24.5 us (2%)
  between operations  15.1 us (1%)
    dynamic_update_slice x48, local copies, waits for them, and re-layouts, ssd_scan(): lax.scan(jax.checkpoint(one_block), start_carry, pieces)  323 us
    psum x1, waiting for transfers between devices, body(): lax.psum((grad_gate_full, grad_inner_full, grad_states_full, grad_step_fu...  223 us
    dot_general x24, matrix products, one_block(): jnp.einsum('hts,shp->thp', mixing, inner_blk, precision=scan_precision)  81.3 us
    psum x1, blocking collectives, body(): lax.psum((grad_gate_full, grad_inner_full, grad_states_full, grad_step_fu...  78.5 us
    dynamic_slice x32, local copies, waits for them, and re-layouts, ssd_scan(): lax.scan(jax.checkpoint(one_block), start_carry, pieces)  49 us
    unnamed x186, local copies, waits for them, and re-layouts  41.4 us
    squeeze x32, local copies, waits for them, and re-layouts, ssd_scan(): lax.scan(jax.checkpoint(one_block), start_carry, pieces)  32.1 us
    another operation x73, other arithmetic  32.1 us
  transfers between devices with their start and end apart: 9, of which 4 were waited for; matrix products, arithmetic and copies ran while one was open for 30% of the time, Pallas kernels for 0%

commit v1 on v0

--- a/solution.py
+++ b/solution.py
@@ -2,7 +2,10 @@
 
 import jax
 import jax.numpy as jnp
+import numpy as np
 from jax import lax
+from jax.experimental import pallas as pl
+from jax.experimental.pallas import tpu as pltpu
 from jax.sharding import PartitionSpec as P
 
 KW = 4
@@ -11,7 +14,7 @@
 
 epsilon = 1e-05
 highest = lax.Precision.HIGHEST
-scan_precision = lax.Precision.HIGH
+INTERPRET = False
 
 
 def round_keep(values):
@@ -39,60 +42,252 @@
     return jax.nn.silu(conv_sum)
 
 
-def ssd_scan(inner_vals, write_vec, read_vec, log_rate, step_size, doc_row, skip_gain):
-    tokens, head_count, head_dim = inner_vals.shape
+def dot_f32(left, right, dims=((1,), (0,))):
+    return lax.dot_general(left, right, (dims, ((), ())), preferred_element_type=jnp.float32)
+
+
+def pair_wide(columns, pair, low_lanes):
+    first = columns[:, 2 * pair : 2 * pair + 1]
+    second = columns[:, 2 * pair + 1 : 2 * pair + 2]
+    return jnp.where(low_lanes, first, second)
+
+
+def decay_of(cum, cum_rows, head, bias):
+    return jnp.exp(cum[:, head : head + 1] - cum_rows[head : head + 1, :] + bias)
+
+
+def mask_bias(doc_col, doc_line):
+    size = doc_col.shape[0]
+    later = lax.broadcasted_iota(jnp.int32, (size, size), 0)
+    earlier = lax.broadcasted_iota(jnp.int32, (size, size), 1)
+    return jnp.where((later >= earlier) & (doc_col == doc_line), 0.0, -1e30)
+
+
+def scan_forward_kernel(
+    inner_ref, write_ref, read_ref, cum_ref, cumrow_ref, enter_ref, tail_ref, step_ref,
+    doccol_ref, docrow_ref, out_ref, state_ref, carried,
+):
+    @pl.when(pl.program_id(0) == 0)
+    def _():
+        carried[...] = jnp.zeros(carried.shape, jnp.float32)
+
+    write, read = write_ref[...], read_ref[...]
+    cum, cum_rows = cum_ref[...], cumrow_ref[...]
+    enter, tail, step = enter_ref[...], tail_ref[...], step_ref[...]
+    size, width = inner_ref.shape
+    pair_lanes = 2 * width // cum.shape[1]
+    low_lanes = lax.broadcasted_iota(jnp.int32, (1, pair_lanes), 1) < pair_lanes // 2
+    bias = mask_bias(doccol_ref[...], docrow_ref[...])
+    scores = dot_f32(read, write, ((1,), (1,)))
+    for pair in range(width // pair_lanes):
+        cols = slice(pair * pair_lanes, (pair + 1) * pair_lanes)
+        stepped = inner_ref[:, cols].astype(jnp.float32) * pair_wide(step, pair, low_lanes)
+        scaled = stepped.astype(jnp.bfloat16)
+        mix_a = (scores * decay_of(cum, cum_rows, 2 * pair, bias)).astype(jnp.bfloat16)
+        mix_b = (scores * decay_of(cum, cum_rows, 2 * pair + 1, bias)).astype(jnp.bfloat16)
+        local = jnp.where(low_lanes, dot_f32(mix_a, scaled), dot_f32(mix_b, scaled))
+        state = carried[:, cols]
+        state_ref[0, :, cols] = state
+        enter_wide = pair_wide(enter, pair, low_lanes)
+        out_ref[:, cols] = local + enter_wide * dot_f32(read, state.astype(jnp.bfloat16))
+        weighted = (scaled.astype(jnp.float32) * pair_wide(tail, pair, low_lanes)).astype(
+            jnp.bfloat16
+        )
+        carried[:, cols] = enter_wide[size - 1 : size, :] * state + dot_f32(
+            write, weighted, ((0,), (0,))
+        )
+
+
+def scan_backward_kernel(
+    inner_ref, write_ref, read_ref, cum_ref, cumrow_ref, enter_ref, tail_ref, step_ref,
+    doccol_ref, docrow_ref, out_ref, state_ref, grad_ref,
+    dinner_ref, dwrite_ref, dread_ref, dcum_ref, dstep_ref, carried,
+):
+    @pl.when(pl.program_id(0) == 0)
+    def _():
+        carried[...] = jnp.zeros(carried.shape, jnp.float32)
+
+    write, read = write_ref[...], read_ref[...]
+    cum, cum_rows = cum_ref[...], cumrow_ref[...]
+    enter, tail, step = enter_ref[...], tail_ref[...], step_ref[...]
+    size, width = inner_ref.shape
+    heads = cum.shape[1]
+    pair_lanes = 2 * width // heads
+    low_lanes = lax.broadcasted_iota(jnp.int32, (1, pair_lanes), 1) < pair_lanes // 2
+    head_lane = lax.broadcasted_iota(jnp.int32, (1, heads), 1)
+    last_row = lax.broadcasted_iota(jnp.int32, (size, 1), 0) == size - 1
+    bias = mask_bias(doccol_ref[...], docrow_ref[...])
+    scores = dot_f32(read, write, ((1,), (1,)))
+    dscores = jnp.zeros((size, size), jnp.float32)
+    dread = jnp.zeros(read.shape, jnp.float32)
+    dwrite = jnp.zeros(write.shape, jnp.float32)
+    dcum = jnp.zeros((size, heads), jnp.float32)
+    dstep = jnp.zeros((size, heads), jnp.float32)
+    for pair in range(width // pair_lanes):
+        cols = slice(pair * pair_lanes, (pair + 1) * pair_lanes)
+        step_wide = pair_wide(step, pair, low_lanes)
+        inner = inner_ref[:, cols].astype(jnp.float32)
+        scaled = (inner * step_wide).astype(jnp.bfloat16)
+        scaled_f = scaled.astype(jnp.float32)
+        grad = grad_ref[:, cols].astype(jnp.bfloat16)
+        grad_f = grad.astype(jnp.float32)
+        decay_a = decay_of(cum, cum_rows, 2 * pair, bias)
+        decay_b = decay_of(cum, cum_rows, 2 * pair + 1, bias)
+        mix_a = (scores * decay_a).astype(jnp.bfloat16)
+        mix_b = (scores * decay_b).astype(jnp.bfloat16)
+        local = jnp.where(
+            low_lanes,
+            dot_f32(mix_a, grad, ((0,), (0,))),
+            dot_f32(mix_b, grad, ((0,), (0,))),
+        )
+        grad_a = jnp.where(low_lanes, grad_f, 0.0).astype(jnp.bfloat16)
+        grad_b = jnp.where(low_lanes, 0.0, grad_f).astype(jnp.bfloat16)
+        dscores = (
+            dscores
+            + dot_f32(grad_a, scaled, ((1,), (1,))) * decay_a
+            + dot_f32(grad_b, scaled, ((1,), (1,))) * decay_b
+        )
+        state = state_ref[0, :, cols]
+        dstate = carried[:, cols]
+        dstate_low = dstate.astype(jnp.bfloat16)
+        tail_wide = pair_wide(tail, pair, low_lanes)
+        enter_wide = pair_wide(enter, pair, low_lanes)
+        enter_end = enter_wide[size - 1 : size, :]
+        from_tail = tail_wide * dot_f32(write, dstate_low)
+        dscaled = local + from_tail
+        entered = (enter_wide * grad_f).astype(jnp.bfloat16)
+        weighted = (scaled_f * tail_wide).astype(jnp.bfloat16)
+        dread = dread + dot_f32(entered, state.astype(jnp.bfloat16), ((1,), (1,)))
+        dwrite = dwrite + dot_f32(weighted, dstate_low, ((1,), (1,)))
+        carried[:, cols] = dot_f32(read, entered, ((0,), (0,))) + enter_end * dstate
+        dinner_ref[:, cols] = dscaled * step_wide
+        row_part = grad_f * out_ref[:, cols] - scaled_f * dscaled
+        end_part = jnp.sum(scaled_f * from_tail, axis=0, keepdims=True) + enter_end * jnp.sum(
+            dstate * state, axis=0, keepdims=True
+        )
+        row_part = row_part + jnp.where(last_row, end_part, 0.0)
+        step_part = dscaled * inner
+        for side in range(2):
+            lanes = low_lanes if side == 0 else jnp.logical_not(low_lanes)
+            own = head_lane == 2 * pair + side
+            row_sum = jnp.sum(jnp.where(lanes, row_part, 0.0), axis=1, keepdims=True)
+            step_sum = jnp.sum(jnp.where(lanes, step_part, 0.0), axis=1, keepdims=True)
+            dcum = dcum + jnp.where(own, row_sum, 0.0)
+            dstep = dstep + jnp.where(own, step_sum, 0.0)
+    dscores_low = dscores.astype(jnp.bfloat16)
+    dread_ref[...] = dread + dot_f32(dscores_low, write)
+    dwrite_ref[...] = dwrite + dot_f32(dscores_low, read, ((0,), (0,)))
+    dcum_ref[...] = dcum
+    dstep_ref[...] = dstep
+
+
+def scan_operands(inner_vals, write_vec, read_vec, log_rate, step_size, doc_row):
+    tokens, heads = log_rate.shape
     blocks = tokens // BLOCK
-    rate_heads = jnp.transpose(log_rate.reshape(blocks, BLOCK, head_count), (0, 2, 1))
-    step_heads = jnp.transpose(step_size.reshape(blocks, BLOCK, head_count), (0, 2, 1))
-    pieces = (
-        inner_vals.reshape(blocks, BLOCK, head_count, head_dim),
-        write_vec.reshape(blocks, BLOCK, -1),
-        read_vec.reshape(blocks, BLOCK, -1),
-        rate_heads,
-        step_heads,
-        doc_row.reshape(blocks, BLOCK),
-    )
-    positions = jnp.arange(BLOCK)
-    lower_tri = positions[:, None] >= positions[None, :]
-
-    def one_block(carry_in, block_data):
-        carried, last_doc = carry_in
-        inner_blk, write_blk, read_blk, rate_blk, step_blk, doc_blk = block_data
-        cumulative = jnp.cumsum(rate_blk, axis=1)
-        allowed = lower_tri & (doc_blk[:, None] == doc_blk[None, :])
-        allowed_wide = allowed[None, :, :]
-        log_gaps = cumulative[:, :, None] - cumulative[:, None, :]
-        decay_mat = jnp.exp(jnp.where(allowed_wide, log_gaps, 0.0)) * allowed_wide.astype(
-            jnp.float32
-        )
-        scores = jnp.dot(read_blk, write_blk.T, precision=scan_precision)
-        mixing = scores[None, :, :] * decay_mat * step_blk[:, None, :]
-        local_out = jnp.einsum("hts,shp->thp", mixing, inner_blk, precision=scan_precision)
-        enter_scale = (doc_blk == last_doc).astype(jnp.float32)[None, :] * jnp.exp(cumulative)
-        from_state = (
-            jnp.einsum("tn,hpn->thp", read_blk, carried, precision=scan_precision)
-            * enter_scale.T[:, :, None]
-        )
-        result = local_out + from_state + skip_gain[None, :, None] * inner_blk
-        final_doc = doc_blk[BLOCK - 1]
-        keep_state = (final_doc == last_doc).astype(jnp.float32)
-        weights_tail = (
-            jnp.exp(cumulative[:, BLOCK - 1 :] - cumulative)
-            * step_blk
-            * (doc_blk == final_doc).astype(jnp.float32)[None, :]
-        )
-        update = jnp.einsum(
-            "hs,shp,sn->hpn", weights_tail, inner_blk, write_blk, precision=scan_precision
-        )
-        carried = keep_state * jnp.exp(cumulative[:, BLOCK - 1])[:, None, None] * carried + update
-        return ((carried, final_doc), result)
-
-    start_carry = (
-        jnp.zeros((head_count, head_dim, write_vec.shape[1]), jnp.float32),
-        jnp.array(-1, jnp.int32),
-    )
-    final_carry, outputs = lax.scan(jax.checkpoint(one_block), start_carry, pieces)
-    return outputs.reshape(tokens, head_count, head_dim)
+    lower = jnp.tril(jnp.ones((BLOCK, BLOCK), jnp.float32))
+    cum = jnp.einsum(
+        "ts,bsh->bth", lower, log_rate.reshape(blocks, BLOCK, heads), precision=highest
+    )
+    doc_blocks = doc_row.reshape(blocks, BLOCK)
+    final = doc_blocks[:, BLOCK - 1]
+    before = jnp.concatenate([jnp.full((1,), -1, jnp.int32), final[:-1]])
+    enter = (doc_blocks == before[:, None]).astype(jnp.float32)[:, :, None] * jnp.exp(cum)
+    tail = (doc_blocks == final[:, None]).astype(jnp.float32)[:, :, None] * jnp.exp(
+        cum[:, BLOCK - 1 :] - cum
+    )
+    flat_cum = cum.reshape(tokens, heads)
+    return (
+        inner_vals.astype(jnp.bfloat16),
+        write_vec.astype(jnp.bfloat16),
+        read_vec.astype(jnp.bfloat16),
+        flat_cum,
+        flat_cum.T,
+        enter.reshape(tokens, heads),
+        tail.reshape(tokens, heads),
+        step_size,
+        doc_row[:, None],
+        doc_row[None, :],
+    )
+
+
+def scan_specs(width, states, heads, place):
+    def rows(columns):
+        return pl.BlockSpec((BLOCK, columns), lambda i: (place(i), 0))
+
+    def lines(count):
+        return pl.BlockSpec((count, BLOCK), lambda i: (0, place(i)))
+
+    return [
+        rows(width), rows(states), rows(states), rows(heads), lines(heads),
+        rows(heads), rows(heads), rows(heads), rows(1), lines(1),
+    ]
+
+
+def scan_call(operands):
+    tokens, width = operands[0].shape
+    states, heads = operands[1].shape[1], operands[3].shape[1]
+    blocks = tokens // BLOCK
+    return pl.pallas_call(
+        scan_forward_kernel,
+        grid=(blocks,),
+        in_specs=scan_specs(width, states, heads, lambda i: i),
+        out_specs=[
+            pl.BlockSpec((BLOCK, width), lambda i: (i, 0)),
+            pl.BlockSpec((1, states, width), lambda i: (i, 0, 0)),
+        ],
+        out_shape=[
+            jax.ShapeDtypeStruct((tokens, width), jnp.float32),
+            jax.ShapeDtypeStruct((blocks, states, width), jnp.float32),
+        ],
+        scratch_shapes=[pltpu.VMEM((states, width), jnp.float32)],
+        interpret=INTERPRET,
+    )(*operands)
+
+
+@jax.custom_vjp
+def ssd_scan(inner_vals, write_vec, read_vec, log_rate, step_size, doc_row):
+    return scan_call(scan_operands(inner_vals, write_vec, read_vec, log_rate, step_size, doc_row))[0]
+
+
+def ssd_keep(*arguments):
+    operands = scan_operands(*arguments)
+    mixed, states_in = scan_call(operands)
+    return mixed, (operands, mixed, states_in)
+
+
+def ssd_back(kept, grad):
+    operands, mixed, states_in = kept
+    tokens, width = mixed.shape
+    blocks, states, _ = states_in.shape
+    heads = operands[3].shape[1]
+
+    def place(i):
+        return blocks - 1 - i
+
+    def rows(columns):
+        return pl.BlockSpec((BLOCK, columns), lambda i: (place(i), 0))
+
+    dinner, dwrite, dread, dcum, dstep = pl.pallas_call(
+        scan_backward_kernel,
+        grid=(blocks,),
+        in_specs=scan_specs(width, states, heads, place)
+        + [rows(width), pl.BlockSpec((1, states, width), lambda i: (place(i), 0, 0)), rows(width)],
+        out_specs=[rows(width), rows(states), rows(states), rows(heads), rows(heads)],
+        out_shape=[
+            jax.ShapeDtypeStruct((tokens, columns), jnp.float32)
+            for columns in (width, states, states, heads, heads)
+        ],
+        scratch_shapes=[pltpu.VMEM((states, width), jnp.float32)],
+        interpret=INTERPRET,
+    )(*operands, mixed, states_in, grad)
+    upper = jnp.triu(jnp.ones((BLOCK, BLOCK), jnp.float32))
+    drate = jnp.einsum(
+        "ut,bth->buh", upper, dcum.reshape(blocks, BLOCK, heads), precision=highest
+    ).reshape(tokens, heads)
+    return dinner, dwrite, dread, drate, dstep, np.zeros((tokens,), jax.dtypes.float0)
+
+
+ssd_scan.defvjp(ssd_keep, ssd_back)
 
 
 def mixer_core(
@@ -118,15 +313,28 @@
     step_size = jax.nn.softplus(step_in + step_bias[None, :])
     log_rate = -jnp.exp(decay_log)[None, :] * step_size
     mixed_out = ssd_scan(
-        inner_vals.reshape(tokens, head_count, -1),
+        inner_vals,
         state_vals[:, :states],
         state_vals[:, states:],
         log_rate,
         step_size,
         doc_row,
-        skip_gain,
-    )
-    return mixed_out.reshape(tokens, -1) * jax.nn.silu(gate_in)
+    )
+    head_dim = inner_vals.shape[1] // head_count
+    mixed_out = mixed_out + jnp.repeat(skip_gain, head_dim)[None, :] * inner_vals
+    return mixed_out * jax.nn.silu(gate_in)
+
+
+def pack(arrays):
+    return jnp.concatenate([array.reshape(-1) for array in arrays])
+
+
+def unpack(flat, arrays):
+    results, start = [], 0
+    for array in arrays:
+        results.append(flat[start : start + array.size].reshape(array.shape))
+        start += array.size
+    return results
 
 
 def body(
@@ -194,7 +402,13 @@
     out_share = lax.psum_scatter(out_part, "col", scatter_dimension=1, tiled=True)
     block_out = (hidden_in.astype(jnp.float32) + out_share).astype(jnp.bfloat16)
     grad_out_full = jnp.einsum(
-        "ti,td->id", normed_out, full_grad, preferred_element_type=jnp.float32
+        "ti,td->di", normed_out, full_grad, preferred_element_type=jnp.float32
+    )
+    out_summed = lax.psum(
+        lax.psum_scatter(
+            grad_out_full.astype(jnp.bfloat16), "row", scatter_dimension=0, tiled=True
+        ),
+        "dp",
     )
     grad_normed_out = jnp.einsum(
         "td,id->ti", full_grad, out_all, preferred_element_type=jnp.float32
@@ -219,13 +433,14 @@
     gate_back = grad_gate.astype(jnp.bfloat16)
     inner_back = grad_inner.astype(jnp.bfloat16)
     step_back = grad_step.astype(jnp.bfloat16)
+    state_back = grad_state.astype(jnp.bfloat16)
     grad_gate_full = jnp.einsum("td,tf->df", normed, gate_back, preferred_element_type=jnp.float32)
     grad_inner_full = jnp.einsum(
         "td,tf->df", normed, inner_back, preferred_element_type=jnp.float32
     )
     grad_step_full = jnp.einsum("td,tf->df", normed, step_back, preferred_element_type=jnp.float32)
     grad_states_full = jnp.einsum(
-        "td,tf->df", normed.astype(jnp.float32), grad_state, precision=highest
+        "td,tf->df", normed, state_back, preferred_element_type=jnp.float32
     )
     grad_normed = jnp.einsum("tf,df->td", gate_back, gate_all, preferred_element_type=jnp.float32)
     grad_normed = grad_normed + jnp.einsum(
@@ -235,69 +450,53 @@
         "tf,df->td", step_back, step_all, preferred_element_type=jnp.float32
     )
     grad_normed = grad_normed + jnp.einsum(
-        "tf,df->td", grad_state, states_all.astype(jnp.float32), precision=highest
+        "tf,df->td", state_back, states_all, preferred_element_type=jnp.float32
     )
     grad_share = lax.psum_scatter(grad_normed, "col", scatter_dimension=1, tiled=True)
     hat_own = hidden_in.astype(jnp.float32) * inv_in
     scaled_in = grad_share * norm_gain.astype(jnp.float32)[None, :]
     grad_norm_gain = jnp.sum(grad_share * hat_own, axis=0)
-    dot_in, grad_states_full, grad_conv_state_weight, grad_conv_state_bias = lax.psum(
-        (
-            jnp.sum(scaled_in * hat_own, axis=1),
-            grad_states_full,
-            grad_conv_state_weight,
-            grad_conv_state_bias,
-        ),
-        "col",
-    )
+    dot_in = lax.psum(jnp.sum(scaled_in * hat_own, axis=1), "col")
     grad_hidden = out_grad.astype(jnp.float32) + inv_in * (
         scaled_in - hat_own * (dot_in / model_width)[:, None]
     )
-    rows_per = proj_gate.shape[0]
-    cols_per = proj_out.shape[1]
-    summed = lax.psum(
-        (
-            grad_gate_full,
-            grad_inner_full,
-            grad_states_full,
-            grad_step_full,
-            grad_out_full,
-            grad_norm_gain,
-            grad_conv_inner_weight,
-            grad_conv_inner_bias,
-            grad_conv_state_weight,
-            grad_conv_state_bias,
-            grad_step_bias,
-            grad_decay_log,
-            grad_skip_gain,
-            grad_gated_gain,
-        ),
-        ("dp", "row"),
-    )
-    row_place = lax.axis_index("row")
-    grad_proj_gate = lax.dynamic_slice_in_dim(summed[0], row_place * rows_per, rows_per, 0)
-    grad_proj_inner = lax.dynamic_slice_in_dim(summed[1], row_place * rows_per, rows_per, 0)
-    grad_proj_states = lax.dynamic_slice_in_dim(summed[2], row_place * rows_per, rows_per, 0)
-    grad_proj_step = lax.dynamic_slice_in_dim(summed[3], row_place * rows_per, rows_per, 0)
-    grad_proj_out = lax.dynamic_slice_in_dim(summed[4], row_place * cols_per, cols_per, 1)
-    smalls = summed[5:]
+    wide = jnp.concatenate(
+        [grad_gate_full, grad_inner_full, grad_states_full, grad_step_full], axis=1
+    ).astype(jnp.bfloat16)
+    wide = lax.psum_scatter(wide, "row", scatter_dimension=0, tiled=True)
+    wide = lax.psum(wide, "dp").astype(jnp.float32)
+    gate_cols, inner_cols = proj_gate.shape[1], proj_inner.shape[1]
+    state_cols = proj_states.shape[1]
+    first, second = gate_cols + inner_cols, gate_cols + inner_cols + state_cols
+    smalls_own = (
+        grad_norm_gain,
+        grad_conv_inner_weight,
+        grad_conv_inner_bias,
+        grad_step_bias,
+        grad_decay_log,
+        grad_skip_gain,
+        grad_gated_gain,
+    )
+    own = unpack(lax.psum(pack(smalls_own), ("dp", "row")), smalls_own)
+    smalls_all = (grad_conv_state_weight, grad_conv_state_bias)
+    shared = unpack(lax.psum(pack(smalls_all), ("dp", "row", "col")), smalls_all)
     return (
         block_out,
         grad_hidden,
-        smalls[0],
-        grad_proj_gate,
-        grad_proj_inner,
-        grad_proj_states,
-        grad_proj_step,
-        smalls[1],
-        smalls[2],
-        smalls[3],
-        smalls[4],
-        smalls[5],
-        smalls[6],
-        smalls[7],
-        smalls[8],
-        grad_proj_out,
+        own[0],
+        wide[:, :gate_cols],
+        wide[:, gate_cols:first],
+        lax.psum(wide[:, first:second], "col"),
+        wide[:, second:],
+        own[1],
+        own[2],
+        shared[0],
+        shared[1],
+        own[3],
+        own[4],
+        own[5],
+        own[6],
+        out_summed.astype(jnp.float32).T,
     )
 
 

time: 1350 us -> 544 us (0.40)
  local copies, waits for them, and re-layouts: 528 us -> 42.1 us
  matrix products: 241 us -> 85.1 us
  waiting for transfers between devices: 247 us -> 101 us
  other arithmetic: 174 us -> 92.4 us
  Pallas kernels: 0 us -> 57.8 us
  blocking collectives: 109 us -> 144 us
  loops' own time: 24.5 us -> 0 us
    dynamic_update_slice x48 -> x0, local copies, waits for them, and re-layouts: 323 us -> none  [ssd_scan(): lax.scan(jax.checkpoint(one_block), start_carry, pieces)]
    psum x2, waiting for transfers between devices: 229 us -> 53.8 us  [the longest x1 53.8 us: body(): wide = lax.psum(wide, 'dp').astype(jnp.float32)]
    dot_general x115 -> x5, matrix products: 185 us -> 22.5 us  [the longest x1 10.1 us: body(): jnp.einsum('tf,df->td', state_back, states_all, preferred_element_type=jn...]
    pallas_call x0 -> x2, Pallas kernels: none -> 57.8 us  [the longest x1 37.8 us: mixer_core(): ssd_scan(inner_vals, state_vals[:, :states], state_vals[:, states:], log_...]
    dynamic_slice x37 -> x0, local copies, waits for them, and re-layouts: 57.1 us -> none  [the longest x32 49 us: ssd_scan(): lax.scan(jax.checkpoint(one_block), start_carry, pieces)]
    psum x2 -> x3, blocking collectives: 82 us -> 118 us  [the longest x1 75.3 us: body(): own = unpack(lax.psum(pack(smalls_own), ('dp', 'row')), smalls_own)]
    unnamed x9 -> x13, waiting for transfers between devices: 3.18 us -> 35.9 us
    squeeze x32 -> x1, local copies, waits for them, and re-layouts: 32.1 us -> 1.43 us  [body(): doc_row = doc_ids[0]]
  transfers between devices with their start and end apart: 9 -> 11, of which waited for: 4 -> 3; matrix products, arithmetic and copies ran while one was open for 30% -> 38% of each run, Pallas kernels for 0% -> 11%
where the time goes in v1:
time: 544 us; the launch traced here: 538 us
  blocking collectives  144 us (26%)
  waiting for transfers between devices  101 us (19%)
  other arithmetic  92.4 us (17%)
  matrix products  85.1 us (16%)
  Pallas kernels  57.8 us (11%)
  local copies, waits for them, and re-layouts  42.1 us (8%)
  between operations  15 us (3%)
    psum x1, blocking collectives, body(): own = unpack(lax.psum(pack(smalls_own), ('dp', 'row')), smalls_own)  75.3 us
    psum x1, waiting for transfers between devices, body(): wide = lax.psum(wide, 'dp').astype(jnp.float32)  53.8 us
    psum x1, blocking collectives, body(): lax.psum(pack(smalls_all), ('dp', 'row', 'col'))  40.1 us
    pallas_call x1, Pallas kernels, mixer_core(): ssd_scan(inner_vals, state_vals[:, :states], state_vals[:, states:], log_...  37.8 us
    unnamed x13, waiting for transfers between devices  35.9 us
    unnamed x146, local copies, waits for them, and re-layouts  24.8 us
    reduce_sum x4, other arithmetic, conv_mix(): weight[taps - 1 - offset][None, :] * shifted * near_masks[offset][:, None]  22.8 us
    pallas_call x1, Pallas kernels, scan_call(): pl.pallas_call(scan_forward_kernel, grid=(blocks,), in_specs=scan_specs(w...  20 us
  transfers between devices with their start and end apart: 11, of which 3 were waited for; matrix products, arithmetic and copies ran while one was open for 38% of the time, Pallas kernels for 11%

profile of v1, /device:TPU:0, one launch (start us, length us, event | category | flops | bytes accessed | tf_op | source)
XLA Modules:
  0.0 538.1 jit_solution(11886608168752661687)
XLA Ops:
  12.7 2.0 all-gather
  16.8 9.5 %all-gather.1 = bf16[4,192,12]{1,2,0:T(8,128)(2,1)S(1)} all-gather(bf16[1,192,12]{1,2,0:T(8,128)(2,1)S(1)} %bitcast.142), channel_id=1, replica_groups=mesh['dp'=4,'row'=4,'col'=2] {'row'}, dimensions={0}, use_global_device_ids=true | all-gather | bytes 23040 | tf_op jit(solution)/shard_map/all_gather | solution.py:369
  26.5 9.5 %all_gather.27 = bf16[768,256]{1,0:T(8,128)(2,1)S(1)} all-gather(bf16[192,256]{1,0:T(8,128)(2,1)S(1)} %copy-done.31), channel_id=1, replica_groups=mesh['dp'=4,'row'=4,'col'=2] {'row'}, dimensions={0}, use_global_device_ids=true | all-gather | bytes 491520 | tf_op jit(solution)/shard_map/all_gather | solution.py:368
  38.9 2.7 fusion
  42.5 2.1 compare_select_fusion.2
  44.6 1.8 convolution_bitcast_fusion.1
  52.0 4.5 fusion.21
  57.6 5.0 fusion.64
  62.7 8.1 %fusion.51 = (bf16[2048,768]{1,0:T(8,128)(2,1)}, f32[2048,768]{1,0:T(8,128)}) fusion(f32[2048]{0:T(1024)S(1)} %get-tuple-element.158, f32[2045,768]{1,0:T(8,128)S(1)} %bitcast.98, f32[768]{0:T(1024)S(1)} %copy-done.35, f32[2048]{0:T(1024)S(1)} %copy-done.28, f32[2046,768]{1,0:T(8,128)S(1)} %bitcast.99, f32[768]{0:T(1024)S(1)} %copy-done.34, ...), kind=kLoop, calls=%fused_computation.137 | loop fusion | flops 31457280 | bytes 34624512 | tf_op jit(solution)/shard_map/jvp()/convert_element_type | solution.py:200
  70.8 20.0 %jvp__.1 = (f32[2048,768]{1,0:T(8,128)}, f32[8,128,768]{2,1,0:T(8,128)}) custom-call(bf16[2048,768]{1,0:T(8,128)(2,1)} %get-tuple-element.130.inner_ref, bf16[2048,128]{1,0:T(8,128)(2,1)} %get-tuple-element.145.write_ref, bf16[2048,128]{1,0:T(8,128)(2,1)} %get-tuple-element.144.read_ref, f32[2048,12]{1,0:T(8,128)} %copy.92.cum_ref, f32[12,2048]{1,0:T(8,128)} %bitcast.122, ...), custom_call_target="tpu_custom_call" | custom-call | tf_op jit(solution)/shard_map/jvp()/pallas_call | solution.py:230
  90.8 13.6 %multiply_reduce_fusion.7 = (f32[2048]{0:T(1024)S(1)}, f32[2048,768]{1,0:T(8,128)}, f32[2048,768]{1,0:T(8,128)}) fusion(f32[2048,768]{1,0:T(8,128)} %get-tuple-element.23.out_ref, f32[2048,768]{1,0:T(8,128)} %get-tuple-element.131, f32[768]{0:T(1024)S(1)} %copy-done.36, bf16[2048,768]{1,0:T(8,128)(2,1)} %copy-done.1, ...), kind=kOutput, calls=%fused_computation.27 | convolution fusion | flops 2442655744 | bytes 29502464 | tf_op jit(solution)/shard_map/dot_general | solution.py:376
  104.4 2.7 psum.56
  107.1 7.7 %fusion.25 = bf16[768,768]{0,1:T(8,128)(2,1)} fusion(bf16[2048,768]{1,0:T(8,128)(2,1)} %all-gather.16.cloned.1.call-done, f32[2048,768]{1,0:T(8,128)} %get-tuple-element.127, f32[768]{0:T(1024)S(1)} %copy-done.48, f32[2048]{0:T(1024)S(1)} %add_rsqrt_fusion), kind=kOutput, calls=%fused_computation.74 | convolution fusion | flops 2421227520 | bytes 10628096 | tf_op jit(solution)/shard_map/ti,td->di/dot_general | solution.py:404
  114.9 2.4 copy.107
  117.3 11.1 %all-gather.14.cloned.1.call-done = bf16[768,768]{0,1:T(8,128)(2,1)} async-done(((bf16[768,192]{0,1:T(8,128)(2,1)}), bf16[768,768]{0,1:T(8,128)(2,1)}) %all-gather.14.cloned.1.call-update) | async-done | bytes 1179664 | tf_op jit(solution)/shard_map/all_gather | solution.py:370
  128.4 9.8 %multiply_reduce_fusion = (f32[768]{0:T(1024)S(1)}, f32[2048]{0:T(1024)S(1)}, f32[2048,768]{1,0:T(8,128)}) fusion(f32[2048,768]{1,0:T(8,128)} %get-tuple-element.127, f32[2048]{0:T(1024)S(1)} %add_rsqrt_fusion, f32[768]{0:T(1024)S(1)} %copy-done.48, bf16[2048,768]{1,0:T(8,128)(2,1)} %all-gather.16.cloned.1.call-done, ...), kind=kOutput, calls=%fused_computation.16 | convolution fusion | flops 2425353472 | bytes 16930816 | tf_op jit(solution)/shard_map/td,id->ti/dot_general | solution.py:413
  138.3 2.8 psum.57
  141.1 17.0 %multiply_reduce_fusion.1 = (f32[768]{0:T(1024)S(1)}, f32[2048,768]{1,0:T(8,128)}, bf16[2048,768]{1,0:T(8,128)(2,1)}) fusion(f32[2048,768]{1,0:T(8,128)} %get-tuple-element.131, f32[2048,768]{1,0:T(8,128)} %get-tuple-element.165, f32[2048]{0:T(1024)S(1)} %broadcast_multiply_fusion.7, f32[2048,768]{1,0:T(8,128)} %get-tuple-element.127, ...), kind=kLoop, calls=%fused_computation.17 | loop fusion | flops 47185152 | bytes 40920064 | tf_op jit(solution)/shard_map/transpose(jvp())/reduce_sum | solution.py:324
  158.1 37.8 %transpose_jvp___.1 = (f32[2048,768]{1,0:T(8,128)}, f32[2048,128]{1,0:T(8,128)}, f32[2048,128]{1,0:T(8,128)}, f32[2048,12]{1,0:T(8,128)}, f32[2048,12]{1,0:T(8,128)}) custom-call(bf16[2048,768]{1,0:T(8,128)(2,1)} %get-tuple-element.130.inner_ref, bf16[2048,128]{1,0:T(8,128)(2,1)} %get-tuple-element.145.write_ref, ...), custom_call_target="tpu_custom_call" | custom-call | tf_op jit(solution)/shard_map/transpose(jvp())/pallas_call | solution.py:315
  195.9 14.4 %multiply_reduce_fusion.5 = (f32[768]{0:T(1024)S(1)}, f32[2048,768]{1,0:T(8,128)}, f32[2048,768]{1,0:T(8,128)}) fusion(f32[2045,768]{1,0:T(8,128)} %bitcast.101, f32[2048]{0:T(1024)S(1)} %get-tuple-element.158, f32[2048,768]{1,0:T(8,128)} %get-tuple-element.131, f32[2048,768]{1,0:T(8,128)} %get-tuple-element.25, f32[2048,768]{1,0:T(8,128)} %get-tuple-element.116.grad_ref, ...), kind=kLoop, calls=%fused_computation.21 | loop fusion | flops 22019328 | bytes 37753856 | tf_op jit(solution)/shard_map/transpose(jvp())/reduce_sum | solution.py:40
  210.3 1.8 convolution_bitcast_fusion
  213.5 2.8 fusion.55
  224.1 3.8 slice_multiply_fusion.2
  230.1 5.8 %multiply_reduce_fusion.4 = (f32[768]{0:T(1024)S(1)}, f32[2048,768]{1,0:T(8,128)}, f32[768]{0:T(1024)S(1)}, f32[2048,768]{1,0:T(8,128)}) fusion(f32[2046,768]{1,0:T(8,128)S(1)} %bitcast.104, f32[2048,768]{1,0:T(8,128)S(1)} %bitcast.113, f32[2048]{0:T(1024)S(1)} %copy-done.28, f32[2047,768]{1,0:T(8,128)S(1)} %bitcast.105, f32[2048]{0:T(1024)S(1)} %copy-done.27), kind=kLoop, calls=%fused_computation.20 | loop fusion | flops 9435648 | bytes 31470592 | tf_op jit(solution)/shard_map/transpose(jvp())/reduce_sum | solution.py:40
  235.9 6.1 %slice_multiply_fusion.1 = f32[2046,768]{1,0:T(8,128)} fusion(f32[2048,768]{1,0:T(8,128)} %get-tuple-element.123, f32[768]{0:T(1024)S(1)} %copy-done.34), kind=kLoop, calls=%fused_computation.14 | loop fusion | flops 1571328 | bytes 12573696 | tf_op jit(solution)/shard_map/transpose(jvp())/mul | solution.py:40
  242.0 3.2 slice_multiply_fusion
  245.3 3.9 convolution_convert_fusion.2
  249.2 7.9 %fusion.52 = (f32[768]{0:T(1024)S(1)}, f32[768]{0:T(1024)S(1)}, bf16[2048,768]{1,0:T(8,128)(2,1)S(1)}) fusion(f32[2048,768]{1,0:T(8,128)S(1)} %bitcast.113, f32[2048,768]{1,0:T(8,128)S(1)} %bitcast.103, f32[768]{0:T(1024)S(1)} %copy-done.32, f32[2047,768]{1,0:T(8,128)} %slice_multiply_fusion, f32[2046,768]{1,0:T(8,128)} %slice_multiply_fusion.1, ...), kind=kLoop, calls=%fused_computation.138 | loop fusion | flops 12581376 | bytes 34593792 | tf_op jit(solution)/shard_map/transpose(jvp())/reduce_sum | solution.py:35
  257.1 1.7 copy-done.15
  258.7 2.9 convolution_convert_fusion.1
  262.0 3.6 copy.105
  265.7 7.6 %fusion.66 = f32[2048,768]{1,0:T(8,128)} fusion(bf16[2048,768]{1,0:T(8,128)(2,1)} %get-tuple-element.132, bf16[768,768]{1,0:T(8,128)(2,1)} %all-gather.12.cloned.1.call-done), kind=kOutput, calls=%fused_computation.147 | convolution fusion | flops 2415919104 | bytes 10616832 | tf_op jit(solution)/shard_map/tf,df->td/dot_general | solution.py:445
  273.2 1.9 copy.108
  275.2 32.7 %reduce-scatter.13.cloned.1.call-done = bf16[192,1804]{1,0:T(8,128)(2,1)} async-done(((bf16[768,1804]{1,0:T(8,128)(2,1)}), bf16[192,1804]{1,0:T(8,128)(2,1)}) %reduce-scatter.13.cloned.1.call-update) | async-done | bytes 692752
  307.9 2.2 copy.106
  310.2 3.5 fusion.34
  313.7 4.5 fusion.67
  318.2 53.8 %all-reduce.30.cloned.1.call-done = (bf16[192,1804]{0,1:T(8,128)(2,1)}, bf16[768,192]{1,0:T(8,128)(2,1)}) async-done(((bf16[192,1804]{0,1:T(8,128)(2,1)}, bf16[768,192]{1,0:T(8,128)(2,1)}), (bf16[192,1804]{0,1:T(8,128)(2,1)}, bf16[768,192]{1,0:T(8,128)(2,1)})) %all-reduce.30.cloned.1.call-update) | async-done | bytes 987664 | tf_op jit(solution)/shard_map/psum | solution.py:467
  372.0 1.6 slice.184
  373.7 10.1 %add_add_fusion = f32[2048,768]{1,0:T(8,128)} fusion(f32[2048,768]{1,0:T(8,128)} %fusion.34, f32[2048,768]{1,0:T(8,128)} %fusion.66, f32[2048,768]{1,0:T(8,128)} %fusion.67, bf16[2048,256]{1,0:T(8,128)(2,1)S(1)} %copy-done.11, bf16[768,256]{1,0:T(8,128)(2,1)S(1)} %copy-done.14), kind=kOutput, calls=%fused_computation.22 | convolution fusion | flops 810024960 | bytes 26607616 | tf_op jit(solution)/shard_map/tf,df->td/dot_general | solution.py:452
  385.1 8.1 %fusion.50 = f32[2048,768]{1,0:T(8,128)} fusion(bf16[768,768]{0,1:T(8,128)(2,1)S(1)} %copy-done.55, f32[2048,768]{1,0:T(8,128)} %get-tuple-element.127, f32[768]{0:T(1024)S(1)} %copy-done.48, f32[2048]{0:T(1024)S(1)} %add_rsqrt_fusion), kind=kOutput, calls=%fused_computation.136 | convolution fusion | flops 2420637696 | bytes 13773824 | tf_op jit(solution)/shard_map/dot_general | solution.py:401
  393.9 40.1 %psum.62 = f32[1280]{0:T(1024)S(1)} all-reduce(f32[1280]{0:T(1024)S(1)} %pad_maximum_fusion.1), channel_id=1, replica_groups=mesh['dp'=4,'row'=4,'col'=2] {'dp','row','col'}, use_global_device_ids=true, to_apply=%region_29.30 | all-reduce | flops 1280 | bytes 10240 | tf_op jit(solution)/shard_map/psum | solution.py:482
  439.2 2.3 copy.98
  441.5 1.7 copy.100
  443.2 2.9 fusion.17
  446.2 75.3 %psum.59 = f32[5028]{0:T(1024)S(1)} all-reduce(f32[5028]{0:T(1024)S(1)} %concatenate.57), channel_id=1, replica_groups=mesh['dp'=4,'row'=4,'col'=2] {'dp','row'}, use_global_device_ids=true, to_apply=%region_20.21 | all-reduce | flops 5028 | bytes 40224 | tf_op jit(solution)/shard_map/psum | solution.py:480
  522.8 2.5 psum.58
  526.5 4.8 fusion.16
  (235 shorter events, 39.3 us)
Async XLA Ops:
  7.2 5.4 %copy-start.57 = (f32[12]{0:T(128)S(1)}, f32[12]{0:T(128)}, u32[]{:S(2)}) copy-start(f32[12]{0:T(128)} %param.29) | copy-start | bytes 148
  7.2 5.4 %copy-start.49 = (bf16[384]{0:T(512)(128)(2,1)S(1)}, bf16[384]{0:T(512)(128)(2,1)}, u32[]{:S(2)}) copy-start(bf16[384]{0:T(512)(128)(2,1)} %param.19) | copy-start | bytes 2308
  7.2 7.5 %copy-start.51 = (f32[4,256]{1,0:T(4,128)S(1)}, f32[4,256]{1,0:T(4,128)}, u32[]{:S(2)}) copy-start(f32[4,256]{1,0:T(4,128)} %param.26) | copy-start | bytes 12292
  7.2 8.2 %copy-start.54 = (f32[12]{0:T(128)S(1)}, f32[12]{0:T(128)}, u32[]{:S(2)}) copy-start(f32[12]{0:T(128)} %param.30) | copy-start | bytes 148
  7.2 9.0 %copy-start.39 = (f32[4,768]{1,0:T(4,128)S(1)}, f32[4,768]{1,0:T(4,128)}, u32[]{:S(2)}) copy-start(f32[4,768]{1,0:T(4,128)} %param.24) | copy-start | bytes 36868
  7.2 9.6 %copy-start.44 = (bf16[192,12]{0,1:T(8,128)(2,1)S(1)}, bf16[192,12]{0,1:T(8,128)(2,1)}, u32[]{:S(2)}) copy-start(bf16[192,12]{0,1:T(8,128)(2,1)} %param.23) | copy-start | bytes 13828
  7.3 19.2 %copy-start.31 = (bf16[192,256]{1,0:T(8,128)(2,1)S(1)}, bf16[192,256]{1,0:T(8,128)(2,1)}, u32[]{:S(2)}) copy-start(bf16[192,256]{1,0:T(8,128)(2,1)} %param.22) | copy-start | bytes 294916
  7.3 31.6 %all-gather.8.cloned.1.call-start = ((), (), s32[]{:S(2)}) async-start(), calls=%async_computation.4 | async-start | bytes 4718592 | tf_op jit(solution)/shard_map/all_gather | solution.py:361
  8.0 49.6 %all-gather.10.cloned.1.call-start = ((), (), s32[]{:S(2)}) async-start(), calls=%async_computation.5 | async-start | bytes 1474560 | tf_op jit(solution)/shard_map/all_gather | solution.py:367
  8.8 82.0 %all-gather.12.cloned.1.call-start = ((), (), s32[]{:S(2)}) async-start(), calls=%async_computation.6 | async-start | bytes 1474560 | tf_op jit(solution)/shard_map/all_gather | solution.py:366
  9.5 97.6 %all-gather.16.cloned.1.call-start = ((), (), s32[]{:S(2)}) async-start(), calls=%async_computation.9 | async-start | bytes 4718592 | tf_op jit(solution)/shard_map/all_gather | solution.py:362
  10.1 118.4 %all-gather.14.cloned.1.call-start = ((), (), s32[]{:S(2)}) async-start(), calls=%async_computation.7 | async-start | bytes 1474560 | tf_op jit(solution)/shard_map/all_gather | solution.py:370
  10.6 262.6 %reduce-scatter.15.cloned.1.call-start = ((), (), s32[]{:S(2)}) async-start(), calls=%async_computation.13 | async-start | bytes 1474560
  12.6 29.8 %copy-start.45 = (f32[12]{0:T(128)}, f32[12]{0:T(128)S(1)}, u32[]{:S(2)}) copy-start(f32[12]{0:T(128)S(1)} %exponential_negate_fusion) | copy-start | bytes 148
  26.5 16.0 %copy-start.25 = (bf16[768,12]{0,1:T(8,128)(2,1)}, bf16[768,12]{0,1:T(8,128)(2,1)S(1)}, u32[]{:S(2)}) copy-start(bf16[768,12]{0,1:T(8,128)(2,1)S(1)} %reshape.239) | copy-start | bytes 55300
  36.0 10.7 %copy-start.13 = (bf16[768,256]{1,0:T(8,128)(2,1)}, bf16[768,256]{1,0:T(8,128)(2,1)S(1)}, u32[]{:S(2)}) copy-start(bf16[768,256]{1,0:T(8,128)(2,1)S(1)} %all_gather.27) | copy-start | bytes 1179652
  47.8 8.7 %copy-start.18 = (f32[2,8,8,256]{3,1,2,0:T(8,128)}, f32[2,8,8,256]{3,1,2,0:T(8,128)S(1)}, u32[]{:S(2)}) copy-start(f32[2,8,8,256]{3,1,2,0:T(8,128)S(1)} %copy.111) | copy-start | bytes 393220
  57.5 5.1 copy-start.28
  57.5 5.1 copy-start.32
  57.5 5.1 copy-start.33
  57.5 5.1 copy-start.34
  57.5 5.1 copy-start.35
  57.5 5.1 copy-start.47
  62.6 8.2 %copy-start = (f32[2048,768]{1,0:T(8,128)}, f32[2048,768]{1,0:T(8,128)S(1)}, u32[]{:S(2)}) copy-start(f32[2048,768]{1,0:T(8,128)S(1)} %fusion.64) | copy-start | bytes 18874372
  70.8 20.0 %copy-start.36 = (f32[768]{0:T(1024)S(1)}, f32[768]{0:T(1024)}, u32[]{:S(2)}) copy-start(f32[768]{0:T(1024)} %mul.508) | copy-start | bytes 9220
  90.8 16.3 %copy-start.48 = (f32[768]{0:T(1024)S(1)}, f32[768]{0:T(1024)}, u32[]{:S(2)}) copy-start(f32[768]{0:T(1024)} %param.31) | copy-start | bytes 9220
  117.3 190.6 %reduce-scatter.13.cloned.1.call-start = ((), (), s32[]{:S(2)}) async-start(), calls=%async_computation.12 | async-start | bytes 3686400
  195.9 14.4 %copy-start.22 = (f32[2048,12]{1,0:T(8,128)S(1)}, f32[2048,12]{1,0:T(8,128)}, u32[]{:S(2)}) copy-start(f32[2048,12]{1,0:T(8,128)} %get-tuple-element.27) | copy-start | bytes 294916
  195.9 14.4 %copy-start.53 = (s32[256]{0:T(256)S(1)}, s32[256]{0:T(256)}, u32[]{:S(2)}) copy-start(s32[256]{0:T(256)} %iota_add_fusion) | copy-start | bytes 3076
  195.9 17.6 %copy-start.46 = (f32[12]{0:T(128)S(1)}, f32[12]{0:T(128)}, u32[]{:S(2)}) copy-start(f32[12]{0:T(128)} %copy-done.45) | copy-start | bytes 148
  222.9 5.2 slice-start.2
  224.1 5.4 %slice-start.1 = ((s8[6291456]{0:T(1024)(128)(4,1)}), s8[2097152]{0:T(1024)(128)(4,1)S(1)}, s32[]{:S(2)}) async-start(s8[6291456]{0:T(1024)(128)(4,1)} %bitcast.102), calls=%async_computation.16 | async-start | bytes 4194304
  224.1 6.0 %slice-start.3 = ((s8[6291456]{0:T(1024)(128)(4,1)}), s8[2097152]{0:T(1024)(128)(4,1)S(1)}, s32[]{:S(2)}) async-start(s8[6291456]{0:T(1024)(128)(4,1)} %bitcast.112), calls=%async_computation.18 | async-start | bytes 4194304
  235.9 6.1 %copy-start.3 = (f32[2048,768]{1,0:T(8,128)S(1)}, f32[2048,768]{1,0:T(8,128)}, u32[]{:S(2)}) copy-start(f32[2048,768]{1,0:T(8,128)} %get-tuple-element.135) | copy-start | bytes 18874372
  265.6 106.4 %all-reduce.30.cloned.1.call-start = ((), (), s32[]{:S(2)}) async-start(), calls=%async_computation.14 | async-start | bytes 2637824 | tf_op jit(solution)/shard_map/psum | solution.py:467
  273.2 36.9 %copy-start.8 = (bf16[2048,12]{1,0:T(8,128)(2,1)S(1)}, bf16[2048,12]{1,0:T(8,128)(2,1)}, u32[]{:S(2)}) copy-start(bf16[2048,12]{1,0:T(8,128)(2,1)} %copy-done.7) | copy-start | bytes 147460
  273.2 36.9 %copy-start.26 = (bf16[768,12]{0,1:T(8,128)(2,1)S(1)}, bf16[768,12]{0,1:T(8,128)(2,1)}, u32[]{:S(2)}) copy-start(bf16[768,12]{0,1:T(8,128)(2,1)} %copy-done.25) | copy-start | bytes 55300
  310.1 131.4 %all-reduce.28.cloned.1.call-start = ((), (), s32[]{:S(2)}) async-start(), calls=%async_computation.11 | async-start | bytes 524288 | tf_op jit(solution)/shard_map/psum | solution.py:489
  313.7 60.0 %copy-start.11 = (bf16[2048,256]{1,0:T(8,128)(2,1)S(1)}, bf16[2048,256]{1,0:T(8,128)(2,1)}, u32[]{:S(2)}) copy-start(bf16[2048,256]{1,0:T(8,128)(2,1)} %copy-done.10) | copy-start | bytes 3145732
  313.7 60.0 %copy-start.14 = (bf16[768,256]{1,0:T(8,128)(2,1)S(1)}, bf16[768,256]{1,0:T(8,128)(2,1)}, u32[]{:S(2)}) copy-start(bf16[768,256]{1,0:T(8,128)(2,1)} %copy-done.13) | copy-start | bytes 1179652
  373.7 69.6 %reduce-scatter.11.cloned.1.call-start = ((), (), s32[]{:S(2)}) async-start(), calls=%async_computation.10 | async-start | bytes 9437184 | tf_op jit(solution)/shard_map/reduce_scatter | solution.py:455
  383.8 142.7 %reduce-scatter.9.cloned.1.call-start = ((), (), s32[]{:S(2)}) async-start(), calls=%async_computation.8 | async-start | bytes 9437184 | tf_op jit(solution)/shard_map/reduce_scatter | solution.py:402
  393.2 42.3 %copy-start.58 = (f32[12]{0:T(128)S(1)}, f32[12]{0:T(128)}, u32[]{:S(2)}) copy-start(f32[12]{0:T(128)} %param.29) | copy-start | bytes 148
  393.2 42.3 %copy-start.12 = (bf16[192,1804]{0,1:T(8,128)(2,1)S(1)}, bf16[192,1804]{0,1:T(8,128)(2,1)}, u32[]{:S(2)}) copy-start(bf16[192,1804]{0,1:T(8,128)(2,1)} %get-tuple-element.106) | copy-start | bytes 2078212
  393.2 42.9 %copy-start.24 = (bf16[768,192]{1,0:T(8,128)(2,1)S(1)}, bf16[768,192]{1,0:T(8,128)(2,1)}, u32[]{:S(2)}) copy-start(bf16[768,192]{1,0:T(8,128)(2,1)} %get-tuple-element.107) | copy-start | bytes 884740
  437.1 6.1 %copy-start.4 = (bf16[2048,384]{1,0:T(8,128)(2,1)S(1)}, bf16[2048,384]{1,0:T(8,128)(2,1)}, u32[]{:S(2)}) copy-start(bf16[2048,384]{1,0:T(8,128)(2,1)} %param.17) | copy-start | bytes 4718596
  437.1 6.1 %copy-start.30 = (f32[2048]{0:T(1024)S(1)}, f32[2048]{0:T(1024)}, u32[]{:S(2)}) copy-start(f32[2048]{0:T(1024)} %copy-done.29) | copy-start | bytes 24580
  439.2 87.3 %copy-start.9 = (bf16[2048,384]{1,0:T(8,128)(2,1)S(1)}, bf16[2048,384]{1,0:T(8,128)(2,1)}, u32[]{:S(2)}) copy-start(bf16[2048,384]{1,0:T(8,128)(2,1)} %param.33) | copy-start | bytes 4718596
  (28 other events, 67.5 us)
Sparse Core Ops, SparseCore 0:
  9.6 14.7 all-gather.7
  26.2 28.7 all-gather.9
  56.9 27.5 all-gather.11
  85.9 12.0 all-gather.15
  99.6 28.7 all-gather.13
  131.2 28.6 reduce-scatter.14
  265.7 42.0 reduce-scatter.12
  310.9 61.0 all-reduce.29
  374.9 17.5 all-reduce.27
  394.7 15.0 reduce-scatter.10
  412.0 15.0 reduce-scatter.8
